TPU v7x, 32 devices: a whole 2x2x4 slice. The times are simulated.
32 devices in a mesh: dp: 2 (over y), expert: 16 (over z, x, core).
Axes of the slice: x: 2, y: 2, z: 4, core: 2. Of those that a mesh axis runs over, the one named last changes fastest.
Arguments:
- tokens: bfloat16 [32768, 768], P(('dp', 'expert')), may hold values from -6 to 6
- routes: int32 [32768, 1], P(('dp', 'expert')), may hold values from 0 to 15
- cotangent: bfloat16 [32768, 768], P(('dp', 'expert')), may hold values from -6 to 6
- gain_first: bfloat16 [768], replicated, may hold values from 0.5 to 1.5
- w_query: bfloat16 [768, 768], replicated, may hold values from -0.21875 to 0.21875
- w_key: bfloat16 [768, 768], replicated, may hold values from -0.21875 to 0.21875
- w_value: bfloat16 [768, 768], replicated, may hold values from -0.21875 to 0.21875
- w_output: bfloat16 [768, 768], replicated, may hold values from -1.75 to 1.75
- bias_table: bfloat16 [32, 12], replicated, may hold values from -4 to 4
- gain_second: bfloat16 [768], replicated, may hold values from 0.5 to 1.5
- w_router: bfloat16 [768, 16], replicated, may hold values from -0.109375 to 0.109375
- expert_in: bfloat16 [16, 768, 3072], P('expert'), may hold values from -0.21875 to 0.21875
- expert_out: bfloat16 [16, 3072, 768], P('expert'), may hold values from -2.5 to 2.5
Outputs:
- out_tokens: bfloat16 [32768, 768], P(('dp', 'expert'))
- grad_tokens: float32 [32768, 768], P(('dp', 'expert'))
- grad_gain_first: float32 [768], replicated
- grad_query: float32 [768, 768], replicated
- grad_key: float32 [768, 768], replicated
- grad_value: float32 [768, 768], replicated
- grad_output: float32 [768, 768], replicated
- grad_table: float32 [32, 12], replicated
- grad_gain_second: float32 [768], replicated
- grad_router: float32 [768, 16], replicated
- grad_expert_in: float32 [16, 768, 3072], P('expert', None, 'dp')
- grad_expert_out: float32 [16, 3072, 768], P('expert', 'dp')
All inputs are finite; a program needn't handle non-finite values.
Results may differ from a plain program's by a relative error of at most 0.015.
Values may be sent and summed in bfloat16 or wider, within the bound.
A program may use at most 320 MiB of HBM per device.

v0:
```python
import jax
import jax.numpy as jnp
from jax import lax
from jax.sharding import PartitionSpec as P

eps_norm = 1e-06
thresholds = (12, 16, 23, 32, 46, 64, 91)


def relative_buckets(query_pos, key_pos):
    offset = key_pos[None, :] - query_pos[:, None]
    distance = jnp.abs(offset)
    far_bucket = 8 + sum(((distance >= threshold).astype(jnp.int32) for threshold in thresholds))
    near_far = jnp.where(distance < 8, distance, far_bucket)
    return near_far + 16 * (offset > 0).astype(jnp.int32)


def rms_norm(values, gain_vector):
    scale = lax.rsqrt(jnp.mean(values * values, axis=-1, keepdims=True) + eps_norm)
    return values * scale * gain_vector


def score_block(query_rows, key_low, bias_table, row_start, scale):
    block_rows = query_rows.shape[0]
    query_pos = row_start + jnp.arange(block_rows, dtype=jnp.int32)
    key_pos = jnp.arange(key_low.shape[0], dtype=jnp.int32)
    buckets = relative_buckets(query_pos, key_pos)
    onehot = (
        buckets[:, :, None] == jnp.arange(bias_table.shape[0], dtype=jnp.int32)[None, None, :]
    ).astype(jnp.bfloat16)
    scores = (
        jnp.einsum("qhd,khd->hqk", query_rows, key_low, preferred_element_type=jnp.float32) * scale
    )
    scores = scores + jnp.einsum(
        "qkb,bh->hqk", onehot, bias_table, preferred_element_type=jnp.float32
    )
    return (scores, onehot)


def local(
    tokens,
    routes,
    cotangent,
    gain_first,
    w_query,
    w_key,
    w_value,
    w_output,
    bias_table,
    gain_second,
    w_router,
    expert_in,
    expert_out,
):
    seq_len, model_width = tokens.shape
    head_count = bias_table.shape[1]
    head_size = model_width // head_count
    experts_all = w_router.shape[1]
    capacity = (5 * seq_len + 4 * experts_all - 1) // (4 * experts_all)
    scale = head_size ** (-0.5)
    block_rows = min(512, seq_len)
    block_count = seq_len // block_rows
    inputs = tokens.astype(jnp.float32)
    normed_one, norm_one_back = jax.vjp(rms_norm, inputs, gain_first.astype(jnp.float32))
    normed_low = normed_one.astype(jnp.bfloat16)
    query_low = (
        jnp.dot(normed_low, w_query, preferred_element_type=jnp.float32)
        .astype(jnp.bfloat16)
        .reshape(seq_len, head_count, head_size)
    )
    key_low = (
        jnp.dot(normed_low, w_key, preferred_element_type=jnp.float32)
        .astype(jnp.bfloat16)
        .reshape(seq_len, head_count, head_size)
    )
    value_low = (
        jnp.dot(normed_low, w_value, preferred_element_type=jnp.float32)
        .astype(jnp.bfloat16)
        .reshape(seq_len, head_count, head_size)
    )
    mixed_parts = []
    lse_parts = []
    for block_index in range(block_count):
        row_start = block_index * block_rows
        query_rows = query_low[row_start : row_start + block_rows]
        scores, onehot = score_block(query_rows, key_low, bias_table, row_start, scale)
        row_max = jnp.max(scores, axis=-1, keepdims=True)
        exp_scores = jnp.exp(scores - row_max)
        row_total = jnp.sum(exp_scores, axis=-1, keepdims=True)
        attn_probs = exp_scores / row_total
        lse_parts.append(row_max + jnp.log(row_total))
        mixed_parts.append(
            jnp.einsum(
                "hqk,khd->qhd",
                attn_probs.astype(jnp.bfloat16),
                value_low,
                preferred_element_type=jnp.float32,
            )
        )
    attn_low = (
        jnp.concatenate(mixed_parts, axis=0).reshape(seq_len, model_width).astype(jnp.bfloat16)
    )
    after_attn = inputs + jnp.dot(attn_low, w_output, preferred_element_type=jnp.float32)
    normed_two, norm_two_back = jax.vjp(rms_norm, after_attn, gain_second.astype(jnp.float32))
    routed_low = normed_two.astype(jnp.bfloat16)
    logits = jnp.dot(routed_low, w_router, preferred_element_type=jnp.float32)
    router_probs = jax.nn.softmax(logits, axis=-1)
    choice_ids = routes[:, 0]
    expert_hot = (choice_ids[:, None] == jnp.arange(experts_all, dtype=jnp.int32)[None, :]).astype(
        jnp.int32
    )
    position = jnp.sum(jnp.cumsum(expert_hot, axis=0) * expert_hot, axis=1) - 1
    slot_hot = position[:, None] == jnp.arange(capacity, dtype=jnp.int32)[None, :]
    dispatch_table = (
        ((expert_hot[:, :, None] > 0) & slot_hot[:, None, :])
        .astype(jnp.bfloat16)
        .reshape(seq_len, experts_all * capacity)
    )
    hot_float = expert_hot.astype(jnp.float32)
    gate_value = jnp.sum(router_probs * hot_float, axis=1)
    slot_rows = jnp.einsum(
        "ts,td->sd", dispatch_table, routed_low, preferred_element_type=jnp.float32
    )
    slot_rows = slot_rows.astype(jnp.bfloat16).reshape(experts_all, 1, capacity, model_width)
    received = lax.all_to_all(slot_rows, "expert", split_axis=0, concat_axis=1, tiled=True)
    hidden_pre = jnp.einsum(
        "esrd,edf->esrf", received, expert_in, preferred_element_type=jnp.float32
    )
    activated = jax.nn.gelu(hidden_pre, approximate=True).astype(jnp.bfloat16)
    produced = jnp.einsum(
        "esrf,efd->esrd", activated, expert_out, preferred_element_type=jnp.float32
    ).astype(jnp.bfloat16)
    returned = lax.all_to_all(produced, "expert", split_axis=1, concat_axis=0, tiled=True)
    returned, hidden_pre, received = (returned, hidden_pre, received)
    combined = jnp.dot(
        dispatch_table,
        returned.reshape(experts_all * capacity, model_width),
        preferred_element_type=jnp.float32,
    )
    output = (after_attn + gate_value[:, None] * combined).astype(jnp.bfloat16)
    upstream = cotangent.astype(jnp.float32)
    gate_grad = jnp.sum(upstream * combined, axis=1)
    token_grad_low = (gate_value[:, None] * upstream).astype(jnp.bfloat16)
    slot_grads = jnp.einsum(
        "ts,td->sd", dispatch_table, token_grad_low, preferred_element_type=jnp.float32
    )
    slot_grads = slot_grads.astype(jnp.bfloat16).reshape(experts_all, 1, capacity, model_width)
    arrived = lax.all_to_all(slot_grads, "expert", split_axis=0, concat_axis=1, tiled=True)
    activated_full, gelu_back = jax.vjp(
        lambda pre_value: jax.nn.gelu(pre_value, approximate=True), hidden_pre
    )
    activated_low = activated_full.astype(jnp.bfloat16)
    act_grad = jnp.einsum("esrd,efd->esrf", arrived, expert_out, preferred_element_type=jnp.float32)
    pre_grad_low = gelu_back(act_grad)[0].astype(jnp.bfloat16)
    input_grad_low = jnp.einsum(
        "esrf,edf->esrd", pre_grad_low, expert_in, preferred_element_type=jnp.float32
    ).astype(jnp.bfloat16)
    sent_back = lax.all_to_all(input_grad_low, "expert", split_axis=1, concat_axis=0, tiled=True)
    full_in = jnp.einsum(
        "esrd,esrf->edf", received, pre_grad_low, preferred_element_type=jnp.float32
    )
    full_out = jnp.einsum(
        "esrf,esrd->efd", activated_low, arrived, preferred_element_type=jnp.float32
    )
    grad_in, grad_out = (
        lax.psum_scatter(
            full_in.astype(jnp.bfloat16), "dp", scatter_dimension=2, tiled=True
        ).astype(jnp.float32),
        lax.psum_scatter(
            full_out.astype(jnp.bfloat16), "dp", scatter_dimension=1, tiled=True
        ).astype(jnp.float32),
    )
    logit_grad_low = ((gate_grad * gate_value)[:, None] * (hot_float - router_probs)).astype(
        jnp.bfloat16
    )
    grad_router = jnp.einsum(
        "td,te->de", routed_low, logit_grad_low, preferred_element_type=jnp.float32
    )
    routed_grad = jnp.dot(
        dispatch_table,
        sent_back.reshape(experts_all * capacity, model_width),
        preferred_element_type=jnp.float32,
    )
    routed_grad = routed_grad + jnp.einsum(
        "te,de->td", logit_grad_low, w_router, preferred_element_type=jnp.float32
    )
    resid_grad, gain_two_grad = norm_two_back(routed_grad)
    after_grad = upstream + resid_grad
    branch_low = after_grad.astype(jnp.bfloat16)
    grad_output_w = jnp.einsum(
        "td,te->de", attn_low, branch_low, preferred_element_type=jnp.float32
    )
    attn_grad_low = jnp.einsum(
        "te,de->td", branch_low, w_output, preferred_element_type=jnp.float32
    )
    attn_grad_low = attn_grad_low.astype(jnp.bfloat16).reshape(seq_len, head_count, head_size)
    query_parts = []
    key_grad = jnp.zeros((seq_len, head_count, head_size), jnp.float32)
    value_grad = jnp.zeros((seq_len, head_count, head_size), jnp.float32)
    table_grad = jnp.zeros(bias_table.shape, jnp.float32)
    for block_index in range(block_count):
        row_start = block_index * block_rows
        query_rows = query_low[row_start : row_start + block_rows]
        scores, onehot = score_block(query_rows, key_low, bias_table, row_start, scale)
        attn_probs = jnp.exp(scores - lse_parts[block_index])
        grad_rows = attn_grad_low[row_start : row_start + block_rows]
        prob_grad = jnp.einsum(
            "qhd,khd->hqk", grad_rows, value_low, preferred_element_type=jnp.float32
        )
        row_dot = jnp.sum(attn_probs * prob_grad, axis=-1, keepdims=True)
        score_grad_low = (attn_probs * (prob_grad - row_dot)).astype(jnp.bfloat16)
        query_parts.append(
            scale
            * jnp.einsum(
                "hqk,khd->qhd", score_grad_low, key_low, preferred_element_type=jnp.float32
            )
        )
        key_grad = key_grad + scale * jnp.einsum(
            "hqk,qhd->khd", score_grad_low, query_rows, preferred_element_type=jnp.float32
        )
        value_grad = value_grad + jnp.einsum(
            "hqk,qhd->khd",
            attn_probs.astype(jnp.bfloat16),
            grad_rows,
            preferred_element_type=jnp.float32,
        )
        table_grad = table_grad + jnp.einsum(
            "qkb,hqk->bh", onehot, score_grad_low, preferred_element_type=jnp.float32
        )
    query_grad_low = (
        jnp.concatenate(query_parts, axis=0).reshape(seq_len, model_width).astype(jnp.bfloat16)
    )
    key_grad_low = key_grad.reshape(seq_len, model_width).astype(jnp.bfloat16)
    value_grad_low = value_grad.reshape(seq_len, model_width).astype(jnp.bfloat16)
    grad_query_w = jnp.einsum(
        "td,te->de", normed_low, query_grad_low, preferred_element_type=jnp.float32
    )
    grad_key_w = jnp.einsum(
        "td,te->de", normed_low, key_grad_low, preferred_element_type=jnp.float32
    )
    grad_value_w = jnp.einsum(
        "td,te->de", normed_low, value_grad_low, preferred_element_type=jnp.float32
    )
    normed_grad = jnp.einsum(
        "te,de->td", query_grad_low, w_query, preferred_element_type=jnp.float32
    )
    normed_grad = normed_grad + jnp.einsum(
        "te,de->td", key_grad_low, w_key, preferred_element_type=jnp.float32
    )
    normed_grad = normed_grad + jnp.einsum(
        "te,de->td", value_grad_low, w_value, preferred_element_type=jnp.float32
    )
    input_resid, gain_one_grad = norm_one_back(normed_grad)
    input_grad = after_grad + input_resid
    summed = lax.psum(
        (
            gain_one_grad,
            grad_query_w,
            grad_key_w,
            grad_value_w,
            grad_output_w,
            table_grad,
            gain_two_grad,
            grad_router,
        ),
        ("dp", "expert"),
    )
    return (
        output,
        input_grad,
        summed[0],
        summed[1],
        summed[2],
        summed[3],
        summed[4],
        summed[5],
        summed[6],
        summed[7],
        grad_in,
        grad_out,
    )


def solution(mesh):
    in_specs = (
        P(("dp", "expert"), None),
        P(("dp", "expert"), None),
        P(("dp", "expert"), None),
        P(),
        P(),
        P(),
        P(),
        P(),
        P(),
        P(),
        P(),
        P("expert", None, None),
        P("expert", None, None),
    )
    out_specs = (
        P(("dp", "expert"), None),
        P(("dp", "expert"), None),
        P(),
        P(),
        P(),
        P(),
        P(),
        P(),
        P(),
        P(),
        P("expert", None, "dp"),
        P("expert", "dp", None),
    )
    return jax.shard_map(local, mesh=mesh, in_specs=in_specs, out_specs=out_specs, check_vma=False)
```

profile of v0, /device:TPU:0, one launch (start us, length us, event | category | flops | bytes accessed | tf_op | source)
XLA Modules:
  0.0 826.7 jit_solution(2873751279195848415)
XLA Ops:
  36.9 16.6 %fusion.3 = f32[512,1024,12]{0,2,1:T(8,128)} fusion(s32[512,1024]{0,1:T(8,128)S(1)} %copy-done.14, bf16[32,12]{0,1:T(8,128)(2,1)S(1)} %copy-done.62), kind=kOutput, calls=%fused_computation.5 | convolution fusion | flops 419430400 | bytes 27263744 | tf_op jit(solution)/shard_map/qkb,bh->hqk/dot_general | solution.py:34
  53.5 30.4 %copy.61 = f32[512,1024,12]{1,0,2:T(8,128)} copy(f32[512,1024,12]{0,2,1:T(8,128)} %fusion.3) | data formatting | bytes 50331648 | tf_op jit(solution)/shard_map/qkb,bh->hqk/dot_general | solution.py:34
  83.9 15.6 %fusion.1 = f32[512,1024,12]{0,2,1:T(8,128)} fusion(s32[512,1024]{0,1:T(8,128)} %fusion.49, bf16[32,12]{0,1:T(8,128)(2,1)S(1)} %copy-done.62), kind=kOutput, calls=%fused_computation.2 | convolution fusion | flops 419430400 | bytes 27263744 | tf_op jit(solution)/shard_map/qkb,bh->hqk/dot_general | solution.py:34
  99.5 30.4 %copy.62 = f32[512,1024,12]{1,0,2:T(8,128)} copy(f32[512,1024,12]{0,2,1:T(8,128)} %fusion.1) | data formatting | bytes 50331648 | tf_op jit(solution)/shard_map/qkb,bh->hqk/dot_general | solution.py:34
  129.9 16.9 %fusion.121 = (f32[12,512]{1,0:T(8,128)}, f32[12,512,1024]{2,1,0:T(8,128)}) fusion(f32[512,1024,12]{1,0,2:T(8,128)} %copy.61, bf16[512,12,64]{0,2,1:T(8,128)(2,1)} %bitcast.171, bf16[1024,12,64]{0,2,1:T(8,128)(2,1)S(1)} %bitcast.165), kind=kOutput, calls=%fused_computation.173 | convolution fusion | flops 824174592 | bytes 52715520 | tf_op jit(solution)/shard_map/qhd,khd->hqk/dot_general | solution.py:32
  146.9 11.1 %fusion.8 = f32[12,512]{1,0:T(8,128)S(1)} fusion(f32[12,512,1024]{2,1,0:T(8,128)} %get-tuple-element.69, f32[12,512]{1,0:T(8,128)} %get-tuple-element.68), kind=kLoop, calls=%fused_computation.24 | loop fusion | flops 12576768 | bytes 25214976 | tf_op jit(solution)/shard_map/reduce_sum | solution.py:89
  158.0 11.3 %fusion.84 = bf16[512,12,64]{0,2,1:T(8,128)(2,1)} fusion(bf16[1024,12,64]{0,2,1:T(8,128)(2,1)S(1)} %bitcast.179, f32[12,512,1024]{2,1,0:T(8,128)} %get-tuple-element.69, f32[12,512]{1,0:T(8,128)S(1)} %fusion.8, f32[12,512]{1,0:T(8,128)S(1)} %copy-done.39), kind=kOutput, calls=%fused_computation.128 | convolution fusion | flops 824573952 | bytes 27574272 | tf_op jit(solution)/shard_map/hqk,khd->qhd/dot_general | solution.py:93
  169.3 17.1 %fusion.120 = (f32[12,512]{1,0:T(8,128)}, f32[12,512,1024]{2,1,0:T(8,128)}) fusion(f32[512,1024,12]{1,0,2:T(8,128)} %copy.62, bf16[512,12,64]{0,2,1:T(8,128)(2,1)S(1)} %bitcast.169, bf16[1024,12,64]{0,2,1:T(8,128)(2,1)S(1)} %bitcast.166), kind=kOutput, calls=%fused_computation.172 | convolution fusion | flops 824174592 | bytes 52715520 | tf_op jit(solution)/shard_map/qhd,khd->hqk/dot_general | solution.py:32
  186.3 11.1 %fusion.9 = f32[12,512]{1,0:T(8,128)S(1)} fusion(f32[12,512,1024]{2,1,0:T(8,128)} %get-tuple-element.67, f32[12,512]{1,0:T(8,128)} %get-tuple-element.66), kind=kLoop, calls=%fused_computation.25 | loop fusion | flops 12576768 | bytes 25214976 | tf_op jit(solution)/shard_map/reduce_sum | solution.py:89
  233.3 30.5 %all-to-all-done = bf16[16,1,80,768]{3,2,1,0:T(8,128)(2,1)} async-done(((bf16[16,1,80,768]{3,2,1,0:T(8,128)(2,1)}), bf16[16,1,80,768]{3,2,1,0:T(8,128)(2,1)}, u32[]{:S(2)}, u32[]{:S(2)}) %all-to-all-start) | async-done | bytes 1966112 | tf_op jit(solution)/shard_map/all_to_all | solution.py:125
  274.6 12.4 %fusion.33 = f32[16,80,3072]{2,1,0:T(8,128)} fusion(bf16[1,768,3072]{2,1,0:T(8,128)(2,1)} %param.24, bf16[16,1,80,768]{3,2,1,0:T(8,128)(2,1)} %all-to-all-done), kind=kOutput, calls=%fused_computation.62 | convolution fusion | flops 6039797760 | bytes 22413312 | tf_op jit(solution)/shard_map/esrd,edf->esrf/dot_general | solution.py:126
  287.0 26.3 %all-to-all-done.2 = bf16[16,1,80,768]{3,2,1,0:T(8,128)(2,1)S(1)} async-done(((bf16[16,1,80,768]{3,2,1,0:T(8,128)(2,1)}), bf16[16,1,80,768]{3,2,1,0:T(8,128)(2,1)S(1)}, u32[]{:S(2)}, u32[]{:S(2)}) %all-to-all-start.2) | async-done | bytes 1966112 | tf_op jit(solution)/shard_map/all_to_all | solution.py:148
  313.4 17.4 %fusion.18 = bf16[16,80,3072]{2,1,0:T(8,128)(2,1)S(1)} fusion(f32[16,80,3072]{2,1,0:T(8,128)} %fusion.33, bf16[1,3072,768]{2,1,0:T(8,128)(2,1)} %param.25, bf16[16,1,80,768]{3,2,1,0:T(8,128)(2,1)S(1)} %all-to-all-done.2), kind=kOutput, calls=%fused_computation.34 | convolution fusion | flops 6118440960 | bytes 30277632 | tf_op jit(solution)/shard_map/esrd,efd->esrf/dot_general | solution.py:153
  343.4 14.8 %convert_bitcast_fusion.1 = bf16[1,16,80,768]{3,2,0,1:T(8,128)(2,1)} fusion(bf16[1,3072,768]{2,1,0:T(8,128)(2,1)} %param.25, f32[16,80,3072]{2,1,0:T(8,128)} %fusion.33), kind=kOutput, calls=%fused_computation.113 | convolution fusion | flops 6076170240 | bytes 22413312 | tf_op jit(solution)/shard_map/esrf,efd->esrd/dot_general | solution.py:130
  358.2 11.3 %all-to-all-start.1 = ((bf16[1,16,80,768]{3,2,0,1:T(8,128)(2,1)}), bf16[1,16,80,768]{3,2,0,1:T(8,128)(2,1)}, u32[]{:S(2)}, u32[]{:S(2)}) async-start(bf16[1,16,80,768]{3,2,0,1:T(8,128)(2,1)} %convert_bitcast_fusion.1), calls=%async_computation.1 | async-start | bytes 3932160 | tf_op jit(solution)/shard_map/all_to_all | solution.py:133
  370.8 11.3 %convert_bitcast_fusion = bf16[1,16,80,768]{3,2,0,1:T(8,128)(2,1)} fusion(bf16[16,80,3072]{2,1,0:T(8,128)(2,1)} %copy-done.67, bf16[1,768,3072]{2,1,0:T(8,128)(2,1)} %param.24), kind=kOutput, calls=%fused_computation.112 | convolution fusion | flops 6040780800 | bytes 14548992 | tf_op jit(solution)/shard_map/esrf,edf->esrd/dot_general | solution.py:155
  382.1 26.3 %all-to-all-done.1 = bf16[1,16,80,768]{3,2,0,1:T(8,128)(2,1)} async-done(((bf16[1,16,80,768]{3,2,0,1:T(8,128)(2,1)}), bf16[1,16,80,768]{3,2,0,1:T(8,128)(2,1)}, u32[]{:S(2)}, u32[]{:S(2)}) %all-to-all-start.1) | async-done | bytes 1966112 | tf_op jit(solution)/shard_map/all_to_all | solution.py:133
  408.4 10.7 %all-to-all-start.3 = ((bf16[1,16,80,768]{3,2,0,1:T(8,128)(2,1)}), bf16[1,16,80,768]{3,2,0,1:T(8,128)(2,1)}, u32[]{:S(2)}, u32[]{:S(2)}) async-start(bf16[1,16,80,768]{3,2,0,1:T(8,128)(2,1)} %convert_bitcast_fusion), calls=%async_computation.3 | async-start | bytes 3932160 | tf_op jit(solution)/shard_map/all_to_all | solution.py:158
  419.2 13.1 %fusion.38 = bf16[1,3072,768]{2,1,0:T(8,128)(2,1)} fusion(bf16[16,1,80,768]{3,2,1,0:T(8,128)(2,1)S(1)} %all-to-all-done.2, f32[16,80,3072]{2,1,0:T(8,128)} %fusion.33), kind=kOutput, calls=%fused_computation.65 | convolution fusion | flops 6077546496 | bytes 22413312 | tf_op jit(solution)/shard_map/esrf,esrd->efd/dot_general | solution.py:162
  439.6 18.4 %all-to-all-done.3 = bf16[1,16,80,768]{3,2,0,1:T(8,128)(2,1)} async-done(((bf16[1,16,80,768]{3,2,0,1:T(8,128)(2,1)}), bf16[1,16,80,768]{3,2,0,1:T(8,128)(2,1)}, u32[]{:S(2)}, u32[]{:S(2)}) %all-to-all-start.3) | async-done | bytes 1966112 | tf_op jit(solution)/shard_map/all_to_all | solution.py:158
  469.1 18.4 %multiply_reduce_fusion.1 = (f32[12,512]{1,0:T(8,128)S(1)}, f32[12,512,1024]{2,1,0:T(8,128)}) fusion(f32[12,512,1024]{2,1,0:T(8,128)} %get-tuple-element.69, f32[12,512]{1,0:T(8,128)S(1)} %copy-done.36, bf16[512,12,64]{0,2,1:T(8,128)(2,1)S(1)} %bitcast.173, bf16[1024,12,64]{0,2,1:T(8,128)(2,1)} %bitcast.177), kind=kOutput, calls=%fused_computation.16 | convolution fusion | flops 824174592 | bytes 52740096 | tf_op jit(solution)/shard_map/qhd,khd->hqk/dot_general | solution.py:207
  487.5 21.5 %multiply_convert_fusion.1 = bf16[12,512,1024]{2,1,0:T(8,128)(2,1)} fusion(f32[12,512,1024]{2,1,0:T(8,128)} %get-tuple-element.80, f32[12,512,1024]{2,1,0:T(8,128)} %get-tuple-element.69, f32[12,512]{1,0:T(8,128)S(1)} %get-tuple-element.79, f32[12,512]{1,0:T(8,128)S(1)} %copy-done.36), kind=kLoop, calls=%fused_computation.15 | loop fusion | flops 25165824 | bytes 62963712 | tf_op jit(solution)/shard_map/convert_element_type | solution.py:211
  509.0 18.9 %multiply_reduce_fusion = (f32[12,512]{1,0:T(8,128)}, f32[12,512,1024]{2,1,0:T(8,128)}) fusion(f32[12,512,1024]{2,1,0:T(8,128)} %get-tuple-element.67, f32[12,512]{1,0:T(8,128)} %log_add_fusion, bf16[512,12,64]{0,2,1:T(8,128)(2,1)S(1)} %bitcast.175, bf16[1024,12,64]{0,2,1:T(8,128)(2,1)} %bitcast.178), kind=kOutput, calls=%fused_computation.13 | convolution fusion | flops 824174592 | bytes 52740096 | tf_op jit(solution)/shard_map/qhd,khd->hqk/dot_general | solution.py:207
  536.4 21.5 %multiply_convert_fusion = bf16[12,512,1024]{2,1,0:T(8,128)(2,1)} fusion(f32[12,512,1024]{2,1,0:T(8,128)} %get-tuple-element.78, f32[12,512,1024]{2,1,0:T(8,128)} %get-tuple-element.67, f32[12,512]{1,0:T(8,128)S(1)} %copy-done.44, f32[12,512]{1,0:T(8,128)S(1)} %copy-done.37), kind=kLoop, calls=%fused_computation.12 | loop fusion | flops 25165824 | bytes 62963712 | tf_op jit(solution)/shard_map/convert_element_type | solution.py:211
  567.8 10.7 %fusion.19 = f32[12,64,1024]{2,1,0:T(8,128)S(1)} fusion(bf16[512,12,64]{0,2,1:T(8,128)(2,1)S(1)} %bitcast.176, f32[12,512,1024]{2,1,0:T(8,128)} %get-tuple-element.67, f32[12,512]{1,0:T(8,128)S(1)} %copy-done.37), kind=kOutput, calls=%fused_computation.36 | convolution fusion | flops 817889280 | bytes 29122560 | tf_op jit(solution)/shard_map/hqk,qhd->khd/dot_general | solution.py:221
  578.6 12.2 %add_convert_fusion = bf16[12,64,1024]{2,1,0:T(8,128)(2,1)} fusion(f32[12,64,1024]{2,1,0:T(8,128)S(1)} %fusion.19, bf16[512,12,64]{0,2,1:T(8,128)(2,1)} %bitcast.174, f32[12,512,1024]{2,1,0:T(8,128)} %get-tuple-element.69, f32[12,512]{1,0:T(8,128)} %log_add_fusion.1), kind=kOutput, calls=%fused_computation.78 | convolution fusion | flops 819462144 | bytes 30695424 | tf_op jit(solution)/shard_map/hqk,qhd->khd/dot_general | solution.py:221
  616.0 23.3 %copy.75 = bf16[12,512,1024]{1,0,2:T(8,128)(2,1)} copy(bf16[12,512,1024]{2,1,0:T(8,128)(2,1)} %multiply_convert_fusion.1) | data formatting | bytes 25165824 | tf_op jit(solution)/shard_map/convert_element_type | solution.py:211
  639.3 23.2 %copy.76 = bf16[12,512,1024]{1,0,2:T(8,128)(2,1)} copy(bf16[12,512,1024]{2,1,0:T(8,128)(2,1)} %multiply_convert_fusion) | data formatting | bytes 25165824 | tf_op jit(solution)/shard_map/convert_element_type | solution.py:211
  677.5 13.1 %fusion.86 = f32[32,12]{0,1:T(8,128)S(1)} fusion(bf16[12,512,1024]{1,0,2:T(8,128)(2,1)} %copy.75, s32[512,1024]{0,1:T(8,128)} %fusion.48), kind=kOutput, calls=%fused_computation.130 | convolution fusion | flops 419430400 | bytes 14681600 | tf_op jit(solution)/shard_map/qkb,hqk->bh/dot_general | solution.py:227
  690.6 13.4 %fusion.88 = f32[32,12]{0,1:T(8,128)S(1)} fusion(f32[32,12]{0,1:T(8,128)S(1)} %fusion.86, bf16[12,512,1024]{1,0,2:T(8,128)(2,1)} %copy.76, s32[512,1024]{0,1:T(8,128)S(1)} %copy-done.15), kind=kOutput, calls=%fused_computation.132 | convolution fusion | flops 419430784 | bytes 14683136 | tf_op jit(solution)/shard_map/qkb,hqk->bh/dot_general | solution.py:227
  704.1 48.0 %all-reduce = (f32[768]{0:T(1024)}, f32[32,12]{0,1:T(8,128)}, f32[768]{0:T(1024)}, f32[768,16]{0,1:T(8,128)}) all-reduce(f32[768]{0:T(1024)S(1)} %get-tuple-element.50, f32[32,12]{0,1:T(8,128)S(1)} %fusion.88, f32[768]{0:T(1024)S(1)} %copy-done.63, f32[768,16]{0,1:T(8,128)S(1)} %fusion.106), channel_id=1, replica_groups=mesh['dp'=2,'expert'=16] {'dp','expert'}, use_global_device_ids=true, to_apply=%region_18.19 | all-reduce | flops 14208 | bytes 113664 | tf_op jit(solution)/shard_map/psum | solution.py:255
  761.0 48.2 %all-reduce.4.cloned.1.call-done = (f32[768,768]{1,0:T(8,128)}, f32[768,768]{1,0:T(8,128)}, f32[768,768]{1,0:T(8,128)}, f32[768,768]{1,0:T(8,128)}) async-done(((f32[768,768]{1,0:T(8,128)}, f32[768,768]{1,0:T(8,128)}, f32[768,768]{1,0:T(8,128)}, f32[768,768]{1,0:T(8,128)}), (f32[768,768]{1,0:T(8,128)}, f32[768,768]{1,0:T(8,128)}, f32[768,768]{1,0:T(8,128)}, ...) | async-done | bytes 9437200 | tf_op jit(solution)/shard_map/psum | solution.py:255
  (230 shorter events, 184.6 us)
Async XLA Ops:
  8.0 22.7 %copy-start = (bf16[768,768]{1,0:T(8,128)(2,1)S(1)}, bf16[768,768]{1,0:T(8,128)(2,1)}, u32[]{:S(2)}) copy-start(bf16[768,768]{1,0:T(8,128)(2,1)} %param.19) | copy-start | bytes 3538948
  10.7 20.0 %copy-start.54 = (f32[768]{0:T(1024)}, f32[768]{0:T(1024)S(1)}, u32[]{:S(2)}) copy-start(f32[768]{0:T(1024)S(1)} %convert_element_type.295) | copy-start | bytes 9220
  27.4 141.8 %copy-start.16 = (bf16[512,768]{0,1:T(8,128)(2,1)}, bf16[512,768]{0,1:T(8,128)(2,1)S(1)}, u32[]{:S(2)}) copy-start(bf16[512,768]{0,1:T(8,128)(2,1)S(1)} %get-tuple-element.65) | copy-start | bytes 2359300
  30.7 138.5 %copy-start.3 = (bf16[1024,768]{0,1:T(8,128)(2,1)}, bf16[1024,768]{0,1:T(8,128)(2,1)S(1)}, u32[]{:S(2)}) copy-start(bf16[1024,768]{0,1:T(8,128)(2,1)S(1)} %convolution_convert_fusion.3) | copy-start | bytes 4718596
  146.8 11.1 %copy-start.19 = (bf16[1024,768]{0,1:T(8,128)(2,1)S(1)}, bf16[1024,768]{0,1:T(8,128)(2,1)}, u32[]{:S(2)}) copy-start(bf16[1024,768]{0,1:T(8,128)(2,1)} %convolution_convert_fusion.5) | copy-start | bytes 4718596
  146.9 11.1 %copy-start.39 = (f32[12,512]{1,0:T(8,128)S(1)}, f32[12,512]{1,0:T(8,128)}, u32[]{:S(2)}) copy-start(f32[12,512]{1,0:T(8,128)} %get-tuple-element.68) | copy-start | bytes 73732
  157.9 11.3 %copy-start.45 = (f32[12,512]{1,0:T(8,128)}, f32[12,512]{1,0:T(8,128)S(1)}, u32[]{:S(2)}) copy-start(f32[12,512]{1,0:T(8,128)S(1)} %fusion.8) | copy-start | bytes 73732
  186.3 11.1 %copy-start.20 = (bf16[1024,768]{0,1:T(8,128)(2,1)S(1)}, bf16[1024,768]{0,1:T(8,128)(2,1)}, u32[]{:S(2)}) copy-start(bf16[1024,768]{0,1:T(8,128)(2,1)} %convolution_convert_fusion.5) | copy-start | bytes 4718596
  186.3 11.1 %copy-start.41 = (f32[12,512]{1,0:T(8,128)S(1)}, f32[12,512]{1,0:T(8,128)}, u32[]{:S(2)}) copy-start(f32[12,512]{1,0:T(8,128)} %get-tuple-element.66) | copy-start | bytes 73732
  213.9 13.7 %copy-start.9 = (bf16[1024,768]{0,1:T(8,128)(2,1)}, bf16[1024,768]{0,1:T(8,128)(2,1)S(1)}, u32[]{:S(2)}) copy-start(bf16[1024,768]{0,1:T(8,128)(2,1)S(1)} %multiply_convert_fusion.4) | copy-start | bytes 4718596
  217.4 46.4 %all-to-all-start = ((bf16[16,1,80,768]{3,2,1,0:T(8,128)(2,1)}), bf16[16,1,80,768]{3,2,1,0:T(8,128)(2,1)}, u32[]{:S(2)}, u32[]{:S(2)}) async-start(bf16[16,1,80,768]{3,2,1,0:T(8,128)(2,1)} %bitcast.185), calls=%async_computation | async-start | bytes 3932160 | tf_op jit(solution)/shard_map/all_to_all | solution.py:125
  227.9 234.5 %copy-start.29 = (f32[1024,16]{0,1:T(8,128)}, f32[1024,16]{0,1:T(8,128)S(1)}, u32[]{:S(2)}) copy-start(f32[1024,16]{0,1:T(8,128)S(1)} %get-tuple-element.73) | copy-start | bytes 196612
  227.9 234.5 %copy-start.47 = (f32[1024]{0:T(1024)}, f32[1024]{0:T(1024)S(1)}, u32[]{:S(2)}) copy-start(f32[1024]{0:T(1024)S(1)} %get-tuple-element.72) | copy-start | bytes 12292
  228.0 234.5 %copy-start.52 = (f32[1024]{0:T(1024)}, f32[1024]{0:T(1024)S(1)}, u32[]{:S(2)}) copy-start(f32[1024]{0:T(1024)S(1)} %fusion.101) | copy-start | bytes 12292
  263.8 49.5 %all-to-all-start.2 = ((bf16[16,1,80,768]{3,2,1,0:T(8,128)(2,1)}), bf16[16,1,80,768]{3,2,1,0:T(8,128)(2,1)S(1)}, u32[]{:S(2)}, u32[]{:S(2)}) async-start(bf16[16,1,80,768]{3,2,1,0:T(8,128)(2,1)} %bitcast.186), calls=%async_computation.2 | async-start | bytes 3932160 | tf_op jit(solution)/shard_map/all_to_all | solution.py:148
  274.5 477.6 %reduce-scatter.3.cloned.1.call-start = ((), (), s32[]{:S(2)}) async-start(), calls=%async_computation.6 | async-start | bytes 7077888 | tf_op jit(solution)/shard_map/reduce_scatter | solution.py:166
  358.2 11.3 %copy-start.40 = (f32[12,512]{1,0:T(8,128)S(1)}, f32[12,512]{1,0:T(8,128)}, u32[]{:S(2)}) copy-start(f32[12,512]{1,0:T(8,128)} %get-tuple-element.68) | copy-start | bytes 73732
  358.2 11.3 %copy-start.46 = (f32[12,512]{1,0:T(8,128)S(1)}, f32[12,512]{1,0:T(8,128)}, u32[]{:S(2)}) copy-start(f32[12,512]{1,0:T(8,128)} %copy-done.45) | copy-start | bytes 73732
  358.2 50.2 %all-to-all-start.1 = ((bf16[1,16,80,768]{3,2,0,1:T(8,128)(2,1)}), bf16[1,16,80,768]{3,2,0,1:T(8,128)(2,1)}, u32[]{:S(2)}, u32[]{:S(2)}) async-start(bf16[1,16,80,768]{3,2,0,1:T(8,128)(2,1)} %convert_bitcast_fusion.1), calls=%async_computation.1 | async-start | bytes 3932160 | tf_op jit(solution)/shard_map/all_to_all | solution.py:133
  408.4 49.6 %all-to-all-start.3 = ((bf16[1,16,80,768]{3,2,0,1:T(8,128)(2,1)}), bf16[1,16,80,768]{3,2,0,1:T(8,128)(2,1)}, u32[]{:S(2)}, u32[]{:S(2)}) async-start(bf16[1,16,80,768]{3,2,0,1:T(8,128)(2,1)} %convert_bitcast_fusion), calls=%async_computation.3 | async-start | bytes 3932160 | tf_op jit(solution)/shard_map/all_to_all | solution.py:158
  419.1 337.5 %reduce-scatter.5.cloned.1.call-start = ((), (), s32[]{:S(2)}) async-start(), calls=%async_computation.7 | async-start | bytes 7077888 | tf_op jit(solution)/shard_map/reduce_scatter | solution.py:169
  432.3 376.9 %all-reduce.4.cloned.1.call-start = ((), (), s32[]{:S(2)}) async-start(), calls=%async_computation.8 | async-start | bytes 18874368 | tf_op jit(solution)/shard_map/psum | solution.py:255
  439.6 22.8 %copy-start.60 = (f32[1024]{0:T(1024)}, f32[1024]{0:T(1024)S(1)}, u32[]{:S(2)}) copy-start(f32[1024]{0:T(1024)S(1)} %mul.288) | copy-start | bytes 12292
  468.5 19.1 %copy-start.18 = (bf16[512,768]{0,1:T(8,128)(2,1)}, bf16[512,768]{0,1:T(8,128)(2,1)S(1)}, u32[]{:S(2)}) copy-start(bf16[512,768]{0,1:T(8,128)(2,1)S(1)} %get-tuple-element.62) | copy-start | bytes 2359300
  509.0 18.9 %copy-start.4 = (bf16[1024,768]{0,1:T(8,128)(2,1)S(1)}, bf16[1024,768]{0,1:T(8,128)(2,1)}, u32[]{:S(2)}) copy-start(bf16[1024,768]{0,1:T(8,128)(2,1)} %copy-done.3) | copy-start | bytes 4718596
  578.5 12.2 %copy-start.8 = (bf16[1024,768]{0,1:T(8,128)(2,1)S(1)}, bf16[1024,768]{0,1:T(8,128)(2,1)}, u32[]{:S(2)}) copy-start(bf16[1024,768]{0,1:T(8,128)(2,1)} %copy-done.5) | copy-start | bytes 4718596
  578.5 12.2 %copy-start.55 = (f32[768]{0:T(1024)S(1)}, f32[768]{0:T(1024)}, u32[]{:S(2)}) copy-start(f32[768]{0:T(1024)} %copy-done.54) | copy-start | bytes 9220
  578.5 12.2 %copy-start.57 = (f32[1024]{0:T(1024)S(1)}, f32[1024]{0:T(1024)}, u32[]{:S(2)}) copy-start(f32[1024]{0:T(1024)} %copy-done.56) | copy-start | bytes 12292
  578.5 19.5 %slice-start.3 = ((s8[12582912]{0:T(1024)(128)(4,1)}), s8[4194304]{0:T(1024)(128)(4,1)S(1)}, s32[]{:S(2)}) async-start(s8[12582912]{0:T(1024)(128)(4,1)} %bitcast.163), calls=%async_computation.12 | async-start | bytes 8388608
  578.5 19.5 %slice-start.4 = ((s8[12582912]{0:T(1024)(128)(4,1)}), s8[4194304]{0:T(1024)(128)(4,1)S(1)}, s32[]{:S(2)}) async-start(s8[12582912]{0:T(1024)(128)(4,1)} %bitcast.163), calls=%async_computation.13 | async-start | bytes 8388608
  677.5 13.1 %copy-start.15 = (s32[512,1024]{0,1:T(8,128)S(1)}, s32[512,1024]{0,1:T(8,128)}, u32[]{:S(2)}) copy-start(s32[512,1024]{0,1:T(8,128)} %fusion.49) | copy-start | bytes 6291460
  690.6 13.5 %copy-start.63 = (f32[768]{0:T(1024)S(1)}, f32[768]{0:T(1024)}, u32[]{:S(2)}) copy-start(f32[768]{0:T(1024)} %get-tuple-element.48) | copy-start | bytes 9220
  (49 other events, 183.6 us)
Sparse Core Ops, SparseCore 0:
  343.5 66.0 reduce-scatter.2
  432.5 61.2 reduce-scatter.4
Sparse Core Ops, SparseCore 1:
  611.3 197.9 all-reduce.3
where the time goes:
time: 837 us; the launch traced here: 827 us
  matrix products  333 us (40%)
  waiting for transfers between devices  150 us (18%)
  local copies, waits for them, and re-layouts  141 us (17%)
  other arithmetic  98.4 us (12%)
  blocking collectives  48 us (6%)
  starting transfers between devices  40.5 us (5%)
  between operations  16.6 us (2%)
    dot_general x2, local copies, waits for them, and re-layouts, score_block(): jnp.einsum('qkb,bh->hqk', onehot, bias_table, preferred_element_type=jnp....  60.8 us
    psum x1, waiting for transfers between devices, local(): lax.psum((gain_one_grad, grad_query_w, grad_key_w, grad_value_w, grad_out...  48.2 us
    psum x1, blocking collectives, local(): lax.psum((gain_one_grad, grad_query_w, grad_key_w, grad_value_w, grad_out...  48 us
    convert_element_type x2, local copies, waits for them, and re-layouts, local(): score_grad_low = (attn_probs * (prob_grad - row_dot)).astype(jnp.bfloat16)  46.5 us
    convert_element_type x2, other arithmetic, local(): score_grad_low = (attn_probs * (prob_grad - row_dot)).astype(jnp.bfloat16)  43 us
    dot_general x2, matrix products, local(): jnp.einsum('qhd,khd->hqk', grad_rows, value_low, preferred_element_type=j...  37.3 us
    dot_general x2, matrix products, score_block(): jnp.einsum('qhd,khd->hqk', query_rows, key_low, preferred_element_type=jn...  34 us
    dot_general x2, matrix products, score_block(): jnp.einsum('qkb,bh->hqk', onehot, bias_table, preferred_element_type=jnp....  32.2 us
  transfers between devices with their start and end apart: 7, of which 5 were waited for; matrix products, arithmetic and copies ran while one was open for 39% of the time, Pallas kernels for 0%

commit v1 on v0

v1 whole, which is shorter than its diff:
```python
import functools

import jax
import jax.numpy as jnp
import numpy as np
from jax import lax
from jax.experimental import pallas as pl
from jax.experimental.pallas import tpu as pltpu
from jax.sharding import PartitionSpec as P

NT = (((1,), (1,)), ((), ()))
NN = (((1,), (0,)), ((), ()))
TN = (((0,), (0,)), ((), ()))


def mm(a, b, dims=NN):
    return lax.dot_general(a, b, dims, preferred_element_type=jnp.float32)


MESH = pl.DeviceIdType.MESH
gelu_a, gelu_b = 0.7978845608028654, 0.044715


def enter(axis_size):
    me, dp = lax.axis_index("expert"), lax.axis_index("dp")
    barrier = pltpu.get_barrier_semaphore()
    for step in range(1, axis_size):
        pl.semaphore_signal(barrier, inc=1, device_id=(dp, me ^ step), device_id_type=MESH)
    pl.semaphore_wait(barrier, axis_size - 1)
    return dp, me


def expert_kernel(
    groups, tile,
    xs_ref, gs_ref, cot_ref, win_ref, wout_ref,
    back_ref, gg_ref, ret_ref, gin_own, gin_oth, gout_own, gout_oth,
    x_scr, c_scr, g_scr, w1, w2, a_scr, p_scr, r_scr, b_scr, e_scr, sq_scr, xt_scr, s32, s16,
    x_send, x_recv, g_send, g_recv, b_send, b_recv, e_send, e_recv, loc, wsem, rsem, osem,
):
    f32, bf16 = jnp.float32, jnp.bfloat16
    n, cap, width = xs_ref.shape
    ff = win_ref.shape[1]
    half = ff // 2
    size = n // groups
    rows = size * cap
    dp, me = enter(n)
    weights = [pltpu.make_async_copy(win_ref, w1, wsem.at[0]), pltpu.make_async_copy(wout_ref, w2, wsem.at[1])]
    own = [
        pltpu.make_async_copy(xs_ref.at[me], x_scr.at[0], loc.at[0]),
        pltpu.make_async_copy(gs_ref.at[me], g_scr.at[0], loc.at[1]),
    ]

    def x_copy(o):
        return pltpu.make_async_remote_copy(xs_ref.at[me ^ o], x_scr.at[o], x_send.at[o], x_recv.at[o], device_id=(dp, me ^ o), device_id_type=MESH)

    def g_copy(o):
        return pltpu.make_async_remote_copy(gs_ref.at[me ^ o], g_scr.at[o], g_send.at[o], g_recv.at[o], device_id=(dp, me ^ o), device_id_type=MESH)

    def b_copy(o):
        return pltpu.make_async_remote_copy(b_scr.at[o], back_ref.at[me], b_send.at[o], b_recv.at[o], device_id=(dp, me ^ o), device_id_type=MESH)

    def e_copy(o):
        return pltpu.make_async_remote_copy(e_scr.at[o], gg_ref.at[me], e_send.at[o], e_recv.at[o], device_id=(dp, me ^ o), device_id_type=MESH)

    def c_copy(o):
        return pltpu.make_async_copy(cot_ref.at[me ^ o], c_scr.at[o], rsem.at[o])

    def r_copy(o):
        return pltpu.make_async_copy(r_scr.at[o], ret_ref.at[me ^ o], rsem.at[o])

    def each(lo, hi, fn):
        if hi - lo <= 4:
            for o in range(lo, hi):
                fn(o)
        else:
            lax.fori_loop(lo, hi, lambda o, c: (fn(o), c)[1], 0)

    for c in weights + own:
        c.start()
    each(1, n, lambda o: x_copy(o).start())
    each(0, n, lambda o: c_copy(o).start())
    each(1, n, lambda o: g_copy(o).start())
    sq_scr[...] = jnp.zeros_like(sq_scr)
    for g in range(groups):
        lo, hi = g * size, (g + 1) * size
        if g == 0:
            for c in own + weights:
                c.wait()
        each(lo, hi, lambda o: c_copy(o).wait())
        each(max(lo, 1), hi, lambda o: x_copy(o).wait_recv())
        x = x_scr[lo:hi].reshape(rows, width)
        ct = c_scr[lo:hi].reshape(rows, width)
        for f in range(0, ff, tile):
            u = mm(x, w1[:, f:f + tile])
            back = mm(ct, w2[f:f + tile, :], NT)
            uu = u * u
            t = jnp.tanh(u * (gelu_a + (gelu_a * gelu_b) * uu))
            hp = 0.5 + 0.5 * t
            a_scr[g * rows:(g + 1) * rows, f:f + tile] = (u * hp).astype(bf16)
            slope = hp + (u * hp) * ((1.0 - t) * (gelu_a + (3.0 * gelu_a * gelu_b) * uu))
            p_scr[g * rows:(g + 1) * rows, f:f + tile] = (back * slope).astype(bf16)
        back = mm(p_scr[g * rows:(g + 1) * rows, :], w1[...], NT)
        b_scr[lo:hi] = back.astype(bf16).reshape(size, cap, width)
        each(max(lo, 1), hi, lambda o: b_copy(o).start())
        r = mm(a_scr[g * rows:(g + 1) * rows, :], w2[...])
        r_scr[lo:hi] = r.astype(bf16).reshape(size, cap, width)
        each(lo, hi, lambda o: r_copy(o).start())
        dots = r * ct.astype(f32)
        part = dots[:, :128]
        for j in range(1, width // 128):
            part = part + dots[:, j * 128:(j + 1) * 128]
        part = part.reshape(size, cap, 128)
        for o in range(lo, hi):
            sq_scr[:cap, :] = part[o - lo]
            line = jnp.sum(sq_scr[...].T, axis=0, keepdims=True)
            e_scr[o] = jnp.broadcast_to(line, (8, 128))
        each(max(lo, 1), hi, lambda o: e_copy(o).start())
    own_back = [
        pltpu.make_async_copy(b_scr.at[0], back_ref.at[me], loc.at[0]),
        pltpu.make_async_copy(e_scr.at[0], gg_ref.at[me], loc.at[1]),
    ]
    for c in own_back:
        c.start()
    each(1, n, lambda o: g_copy(o).wait_recv())

    def gated(o):
        col = jnp.broadcast_to(g_scr[o][:1, :], (128, 128)).T[:cap, :1]
        x_scr[o] = (x_scr[o].astype(f32) * col).astype(bf16)
        c_scr[o] = (c_scr[o].astype(f32) * col).astype(bf16)

    each(0, n, gated)
    total = n * cap
    xt_scr[...] = x_scr[...].reshape(total, width).T
    ct = c_scr[...].reshape(total, width)
    count = half // tile
    pend = {}
    step = 0
    for t in range(count):
        for mine in (True, False):
            start = pl.multiple_of((dp if mine else 1 - dp) * half + t * tile, 128)
            stage = s32 if mine else s16
            slot = t % 2
            outs = (gin_own, gout_own) if mine else (gin_oth, gout_oth)
            if (mine, slot) in pend:
                for c in pend[(mine, slot)]:
                    c.wait()
            gin = mm(xt_scr[...], p_scr[:, pl.ds(start, tile)])
            gout = lax.dot_general(a_scr[:, pl.ds(start, tile)], ct, TN, preferred_element_type=f32)
            stage[0][slot] = gin.astype(stage[0].dtype)
            stage[1][slot] = gout.astype(stage[1].dtype)
            k = (0 if mine else 4) + slot * 2
            cs = [
                pltpu.make_async_copy(stage[0].at[slot], outs[0].at[:, t * tile:(t + 1) * tile], osem.at[k]),
                pltpu.make_async_copy(stage[1].at[slot], outs[1].at[t * tile:(t + 1) * tile, :], osem.at[k + 1]),
            ]
            for c in cs:
                c.start()
            pend[(mine, slot)] = cs
    for cs in pend.values():
        for c in cs:
            c.wait()
    for c in own_back:
        c.wait()
    each(0, n, lambda o: r_copy(o).wait())
    each(1, n, lambda o: x_copy(o).wait_send())
    each(1, n, lambda o: g_copy(o).wait_send())
    each(1, n, lambda o: b_copy(o).wait())
    each(1, n, lambda o: e_copy(o).wait())


def expert_pass(xs, gs, cot, w_in, w_out, groups=4):
    f32, bf16 = jnp.float32, jnp.bfloat16
    n, cap, width = xs.shape
    ff = w_in.shape[1]
    half = ff // 2
    tile = 512 if n * cap <= 1280 else 256
    hbm = pl.BlockSpec(memory_space=pl.ANY)
    dma = pltpu.SemaphoreType.DMA
    flat = jax.ShapeDtypeStruct((n, cap, width), bf16)
    return pl.pallas_call(
        functools.partial(expert_kernel, groups, tile),
        in_specs=[hbm] * 5,
        out_specs=[hbm] * 7,
        out_shape=[
            flat, jax.ShapeDtypeStruct((n, 8, 128), f32), flat,
            jax.ShapeDtypeStruct((width, half), f32), jax.ShapeDtypeStruct((width, half), bf16),
            jax.ShapeDtypeStruct((half, width), f32), jax.ShapeDtypeStruct((half, width), bf16),
        ],
        scratch_shapes=[
            pltpu.VMEM((n, cap, width), bf16), pltpu.VMEM((n, cap, width), bf16), pltpu.VMEM((n, 8, 128), f32),
            pltpu.VMEM((width, ff), bf16), pltpu.VMEM((ff, width), bf16),
            pltpu.VMEM((n * cap, ff), bf16), pltpu.VMEM((n * cap, ff), bf16),
            pltpu.VMEM((n, cap, width), bf16), pltpu.VMEM((n, cap, width), bf16), pltpu.VMEM((n, 8, 128), f32),
            pltpu.VMEM((128, 128), f32), pltpu.VMEM((width, n * cap), bf16),
            [pltpu.VMEM((2, width, tile), f32), pltpu.VMEM((2, tile, width), f32)],
            [pltpu.VMEM((2, width, tile), bf16), pltpu.VMEM((2, tile, width), bf16)],
        ] + [dma((n,))] * 8 + [dma((2,)), dma((2,)), dma((n,)), dma((8,))],
        compiler_params=pltpu.CompilerParams(collective_id=1, has_side_effects=True, vmem_limit_bytes=62 << 20),
        name="experts",
    )(xs, gs, cot, w_in, w_out)

def swap_copy(src, dst, send, recv, dp, me, o):
    return pltpu.make_async_remote_copy(src.at[me ^ o], dst.at[me], send.at[o], recv.at[o], device_id=(dp, me ^ o), device_id_type=MESH)


def swap_start(src, dst, send, recv, loc):
    n = src.shape[0]
    dp, me = enter(n)
    pltpu.make_async_copy(src.at[me], dst.at[me], loc.at[0]).start()
    for o in range(1, n):
        swap_copy(src, dst, send, recv, dp, me, o).start()


def swap_wait(src, dst, send, recv, loc):
    n = src.shape[0]
    dp, me = lax.axis_index("dp"), lax.axis_index("expert")
    pltpu.make_async_copy(src.at[me], dst.at[me], loc.at[0]).wait()
    for o in range(1, n):
        swap_copy(src, dst, send, recv, dp, me, o).wait()


def fwd_kernel(rows, g_ref, q_ref, k_ref, v_ref, cs_ref, o_ref, p_ref, cr_ref, b_scr, send, recv, loc):
    seq = q_ref.shape[0]
    blocks = seq // 128
    step = pl.program_id(0)

    @pl.when(step == 0)
    def _():
        swap_start(cs_ref, cr_ref, send, recv, loc)

    lane = lax.broadcasted_iota(jnp.int32, (rows, 128), 1)
    for hh in range(2):
        own = (lane >= 64) if hh else (lane < 64)
        g = g_ref[0, hh:hh + 1, :]
        near = pltpu.roll(jnp.broadcast_to(g, (128, 512)), 384, axis=1, stride=1, stride_axis=0)
        mid = (blocks - 2) * 128
        b_scr[:, :mid] = jnp.broadcast_to(g[:, :1], (128, mid))
        b_scr[:, mid:mid + 384] = near[:, :384]
        b_scr[:, mid + 384:] = jnp.broadcast_to(g[:, 511:], (128, b_scr.shape[1] - mid - 384))
        for i in range(seq // rows):
            r0 = i * rows
            q = q_ref[r0:r0 + rows, :]
            qm = jnp.where(own, q * jnp.bfloat16(0.125), jnp.bfloat16(0))
            s = mm(qm, k_ref[...], NT)
            parts = []
            for a in range(rows // 128):
                c0 = (blocks - 1 - (r0 // 128 + a)) * 128
                parts.append(s[a * 128:(a + 1) * 128] + b_scr[:, c0:c0 + seq])
            s = jnp.concatenate(parts, 0) if len(parts) > 1 else parts[0]
            m = jnp.max(s, axis=-1, keepdims=True)
            e = jnp.exp(s - m)
            inv = 1.0 / jnp.sum(e, axis=-1, keepdims=True)
            p = (e * inv).astype(jnp.bfloat16)
            p_ref[hh, r0:r0 + rows, :] = p
            o = mm(p, v_ref[...]).astype(jnp.bfloat16)
            if hh == 0:
                o_ref[r0:r0 + rows, :] = o
            else:
                o_ref[r0:r0 + rows, :] = jnp.where(own, o, o_ref[r0:r0 + rows, :])

    @pl.when(step == pl.num_programs(0) - 1)
    def _():
        swap_wait(cs_ref, cr_ref, send, recv, loc)


def attn_fwd(gvec, q, k, v, cs, rows=256):
    seq, width = q.shape
    pairs = width // 128
    n = cs.shape[0]
    col = pl.BlockSpec((seq, 128), lambda h: (0, h))
    hbm = pl.BlockSpec(memory_space=pl.ANY)
    dma = pltpu.SemaphoreType.DMA
    return pl.pallas_call(
        functools.partial(fwd_kernel, rows),
        grid=(pairs,),
        in_specs=[pl.BlockSpec((1, 2, 512), lambda h: (h, 0, 0)), col, col, col, hbm],
        out_specs=[col, pl.BlockSpec((2, seq, seq), lambda h: (h, 0, 0)), hbm],
        out_shape=[
            jax.ShapeDtypeStruct((seq, width), jnp.bfloat16),
            jax.ShapeDtypeStruct((2 * pairs, seq, seq), jnp.bfloat16),
            jax.ShapeDtypeStruct(cs.shape, cs.dtype),
        ],
        scratch_shapes=[pltpu.VMEM((128, 2 * seq - 128), jnp.float32), dma((n,)), dma((n,)), dma((1,))],
        compiler_params=pltpu.CompilerParams(
            dimension_semantics=("arbitrary",), collective_id=3, has_side_effects=True, vmem_limit_bytes=48 << 20
        ),
        name="attn_fwd",
    )(gvec, q, k, v, cs)


def bwd_kernel(
    rows, q_ref, k_ref, v_ref, o_ref, d_ref, p_ref, x_ref, a_ref, br_ref, wq_ref, wk_ref, wv_ref, rs_ref,
    near_ref, far_ref, dw_ref, ng_ref, rr_ref,
    ds_scr, qt_scr, dt_scr, near_scr, far_scr, xt_scr, at_scr, dz_scr, send, recv, loc,
):
    seq = q_ref.shape[0]
    blocks = seq // 128
    step = pl.program_id(0)

    @pl.when(step == 0)
    def _():
        swap_start(rs_ref, rr_ref, send, recv, loc)
        xt_scr[...] = x_ref[...].T
        at_scr[...] = a_ref[...].T

    lane = lax.broadcasted_iota(jnp.int32, (rows, 128), 1)
    sub = lax.broadcasted_iota(jnp.int32, (128, seq), 0)
    qt = q_ref[...].T
    dt = d_ref[...].T
    zero = jnp.bfloat16(0)
    for hh in range(2):
        half = (sub >= 64) if hh else (sub < 64)
        qt_scr[:, hh * seq:(hh + 1) * seq] = jnp.where(half, qt, zero)
        dt_scr[:, hh * seq:(hh + 1) * seq] = jnp.where(half, dt, zero)
    for hh in range(2):
        own = (lane >= 64) if hh else (lane < 64)
        near_scr[...] = jnp.zeros_like(near_scr)
        far_scr[...] = jnp.zeros_like(far_scr)
        for i in range(seq // rows):
            r0 = i * rows
            d = jnp.where(own, d_ref[r0:r0 + rows, :], zero)
            dp = mm(d, v_ref[...], NT)
            delta = jnp.sum(d.astype(jnp.float32) * o_ref[r0:r0 + rows, :].astype(jnp.float32), axis=-1, keepdims=True)
            ds = p_ref[hh, r0:r0 + rows, :].astype(jnp.float32) * (dp - delta)
            low = ds.astype(jnp.bfloat16)
            ds_scr[hh * seq + r0:hh * seq + r0 + rows, :] = low
            for a in range(rows // 128):
                bi = r0 // 128 + a
                strip = ds[a * 128:(a + 1) * 128]
                lo, hi = max(bi - 1, 0), min(bi + 2, blocks)
                near_scr[:, (lo - bi + 1) * 128:(hi - bi + 1) * 128] += strip[:, lo * 128:hi * 128]
                if lo > 0:
                    t = strip[:, :128]
                    for j in range(1, lo):
                        t = t + strip[:, j * 128:(j + 1) * 128]
                    far_scr[:, :128] += t
                if hi < blocks:
                    t = strip[:, hi * 128:(hi + 1) * 128]
                    for j in range(hi + 1, blocks):
                        t = t + strip[:, j * 128:(j + 1) * 128]
                    far_scr[:, 128:] += t
            dq = (0.125 * mm(low, k_ref[...])).astype(jnp.bfloat16)
            if hh == 0:
                dz_scr[r0:r0 + rows, :128] = dq
            else:
                dz_scr[r0:r0 + rows, :128] = jnp.where(own, dq, dz_scr[r0:r0 + rows, :128])
        a = near_scr[...]
        n = 128
        while n > 8:
            n //= 2
            a = a[:n] + pltpu.roll(a[n:], 512 - n, axis=1)
        near_ref[0, hh * 8:(hh + 1) * 8, :] = a
        f = far_scr[...]
        n = 128
        while n > 8:
            n //= 2
            f = f[:n] + f[n:]
        far_ref[0, hh * 8:(hh + 1) * 8, :] = f
    dkt = mm(qt_scr[...], ds_scr[...])
    dz_scr[:, 128:256] = (0.125 * dkt).astype(jnp.bfloat16).T
    dvt = mm(dt_scr[...], p_ref[...].reshape(2 * seq, seq))
    dz_scr[:, 256:] = dvt.astype(jnp.bfloat16).T
    dz = dz_scr[...]
    dw = mm(xt_scr[...], dz).astype(jnp.bfloat16)
    for j in range(3):
        dw_ref[0, j] = dw[:, j * 128:(j + 1) * 128]
    dw_ref[0, 3] = mm(at_scr[...], br_ref[...]).astype(jnp.bfloat16)
    w = jnp.concatenate([wq_ref[...], wk_ref[...], wv_ref[...]], axis=1)
    ng = mm(dz, w, NT)

    @pl.when(step == 0)
    def _():
        ng_ref[...] = ng

    @pl.when(step > 0)
    def _():
        ng_ref[...] += ng

    @pl.when(step == pl.num_programs(0) - 1)
    def _():
        swap_wait(rs_ref, rr_ref, send, recv, loc)


def attn_bwd(q, k, v, o, d, p, x, branch, wq, wk, wv, rs, rows=256):
    f32, bf16 = jnp.float32, jnp.bfloat16
    seq, width = q.shape
    pairs = width // 128
    n = rs.shape[0]
    col = pl.BlockSpec((seq, 128), lambda h: (0, h))
    wcol = pl.BlockSpec((width, 128), lambda h: (0, h))
    full = pl.BlockSpec((seq, width), lambda h: (0, 0))
    hbm = pl.BlockSpec(memory_space=pl.ANY)
    dma = pltpu.SemaphoreType.DMA
    return pl.pallas_call(
        functools.partial(bwd_kernel, rows),
        grid=(pairs,),
        in_specs=[col] * 5 + [pl.BlockSpec((2, seq, seq), lambda h: (h, 0, 0)), full, full, col] + [wcol] * 3 + [hbm],
        out_specs=[
            pl.BlockSpec((1, 16, 512), lambda h: (h, 0, 0)),
            pl.BlockSpec((1, 16, 256), lambda h: (h, 0, 0)),
            pl.BlockSpec((1, 4, width, 128), lambda h: (h, 0, 0, 0)),
            full,
            hbm,
        ],
        out_shape=[
            jax.ShapeDtypeStruct((pairs, 16, 512), f32),
            jax.ShapeDtypeStruct((pairs, 16, 256), f32),
            jax.ShapeDtypeStruct((pairs, 4, width, 128), bf16),
            jax.ShapeDtypeStruct((seq, width), f32),
            jax.ShapeDtypeStruct(rs.shape, rs.dtype),
        ],
        scratch_shapes=[
            pltpu.VMEM((2 * seq, seq), bf16), pltpu.VMEM((128, 2 * seq), bf16), pltpu.VMEM((128, 2 * seq), bf16),
            pltpu.VMEM((128, 512), f32), pltpu.VMEM((128, 256), f32),
            pltpu.VMEM((width, seq), bf16), pltpu.VMEM((width, seq), bf16), pltpu.VMEM((seq, 384), bf16),
            dma((n,)), dma((n,)), dma((1,)),
        ],
        compiler_params=pltpu.CompilerParams(
            dimension_semantics=("arbitrary",), collective_id=4, has_side_effects=True, vmem_limit_bytes=56 << 20
        ),
        name="attn_bwd",
    )(q, k, v, o, d, p, x, o, branch, wq, wk, wv, rs)

def reduce_kernel(main_ref, small_ref, out_q, out_k, out_v, out_o, small_out, acc, rbuf, obuf, s_acc, s_rbuf, s_obuf, send, recv, s_send, s_recv):
    f32, bf16 = jnp.float32, jnp.bfloat16
    chunks, total, rows, _ = main_ref.shape
    n = total // 2
    me, dp = lax.axis_index("expert"), lax.axis_index("dp")
    bits = n.bit_length() - 1
    peers = [((dp, me ^ (1 << b)), (me >> b) & 1) for b in range(bits)] + [((1 - dp, me), dp)]
    barrier = pltpu.get_barrier_semaphore()
    for dev, _ in peers:
        pl.semaphore_signal(barrier, inc=1, device_id=dev, device_id_type=MESH)
    pl.semaphore_wait(barrier, len(peers))
    stages = bits + 1
    base = list(range(stages))
    orders = [base, [0] + base[2:bits] + [1, bits], [0, bits] + base[1:bits]]
    lanes = [(c, main_ref.at[c], acc.at[c], rbuf.at[c], obuf.at[c], send.at[c], recv.at[c], orders[c % 3], bf16) for c in range(chunks)]
    lanes.append((chunks, small_ref, s_acc, s_rbuf, s_obuf, s_send, s_recv, orders[2], f32))
    spans = {c: [] for c in range(chunks + 1)}
    start = {c: 0 for c in range(chunks + 1)}

    def halve(lane, s):
        c, source, mine, inbox, _, ss, rs, order, _ = lane
        dev, own = peers[order[s]]
        size = total >> (s + 1)
        keep = start[c] + own * size
        give = start[c] + (1 - own) * size
        spans[c].append(keep)
        start[c] = keep
        now = source if s == 0 else mine
        off = total - 2 * size
        return pltpu.make_async_remote_copy(now.at[pl.ds(give, size)], inbox.at[pl.ds(off, size)], ss.at[s], rs.at[s], device_id=dev, device_id_type=MESH)

    def fold(lane, s):
        c, source, mine, inbox, outbox, _, _, _, kind = lane
        size = total >> (s + 1)
        now = source if s == 0 else mine
        off = total - 2 * size
        keep = spans[c][s]
        goal = outbox if s == stages - 1 else mine

        def one(j, _):
            goal[keep + j] = (now[keep + j].astype(f32) + inbox[off + j].astype(f32)).astype(kind)
            return 0

        lax.fori_loop(0, size, one, 0)

    def double(lane, s):
        c, _, _, _, outbox, ss, rs, order, _ = lane
        dev, _ = peers[order[s]]
        size = total >> (s + 1)
        piece = outbox.at[pl.ds(spans[c][s], size)]
        k = 2 * stages - 1 - s
        return pltpu.make_async_remote_copy(piece, piece, ss.at[k], rs.at[k], device_id=dev, device_id_type=MESH)

    live = {}
    for s in range(stages):
        for lane in lanes:
            if s:
                live[lane[0]].wait()
                fold(lane, s - 1)
            live[lane[0]] = halve(lane, s)
            live[lane[0]].start()
    for s in reversed(range(stages)):
        for lane in lanes:
            live[lane[0]].wait()
            if s == stages - 1:
                fold(lane, s)
            live[lane[0]] = double(lane, s)
            live[lane[0]].start()
    outs = (out_q, out_k, out_v, out_o)
    depth, width = out_q.shape
    per = depth // rows
    tiles = 4 * (width // 128)
    for c in range(chunks):
        live[c].wait()
        share = tiles // chunks
        for j in range(share):
            t = c * share + j
            out = outs[t % 4]
            out[:, (t // 4) * 128:(t // 4 + 1) * 128] = obuf[c, j * per:(j + 1) * per].reshape(depth, 128).astype(f32)
    live[chunks].wait()
    small_out[...] = s_obuf[...]


def reduce_all(main, small, width):
    f32, bf16 = jnp.float32, jnp.bfloat16
    chunks, total, rows, _ = main.shape
    stages = total.bit_length() - 1
    vm = pl.BlockSpec(memory_space=pltpu.VMEM)
    dma = pltpu.SemaphoreType.DMA
    square = jax.ShapeDtypeStruct((width, width), f32)
    buf, sbuf = pltpu.VMEM(main.shape, bf16), pltpu.VMEM(small.shape, f32)
    return pl.pallas_call(
        reduce_kernel,
        in_specs=[vm, vm],
        out_specs=[vm] * 5,
        out_shape=[square] * 4 + [jax.ShapeDtypeStruct(small.shape, f32)],
        scratch_shapes=[buf, buf, buf, sbuf, sbuf, sbuf, dma((chunks, 2 * stages)), dma((chunks, 2 * stages)), dma((2 * stages,)), dma((2 * stages,))],
        compiler_params=pltpu.CompilerParams(collective_id=2, has_side_effects=True, vmem_limit_bytes=40 << 20),
        name="reduce_all",
    )(main, small)

eps_norm = 1e-06
thresholds = (12, 16, 23, 32, 46, 64, 91)


def bucket_of(offset):
    distance = np.abs(offset)
    far = 8 + sum((distance >= t).astype(np.int32) for t in thresholds)
    return np.where(distance < 8, distance, far) + 16 * (offset > 0)


def hot_of(offset):
    return (bucket_of(offset)[..., None] == np.arange(32)).astype(np.float32)


def local(dp_count, tokens, routes, cotangent, gain_first, w_query, w_key, w_value, w_output, bias_table, gain_second, w_router, expert_in, expert_out):
    f32, bf16 = jnp.float32, jnp.bfloat16
    seq, width = tokens.shape
    heads = bias_table.shape[1]
    experts = w_router.shape[1]
    cap = (5 * seq + 4 * experts - 1) // (4 * experts)
    capp = (cap + 15) // 16 * 16
    slots = experts * capp
    ids = routes[:, 0]
    hot = (ids[:, None] == jnp.arange(experts, dtype=jnp.int32)[None, :]).astype(bf16)
    order = jnp.arange(seq, dtype=jnp.int32)
    before = (order[:, None] > order[None, :]).astype(bf16)
    hot32 = hot.astype(f32)
    position = jnp.sum(mm(before, hot) * hot32, axis=1).astype(jnp.int32)
    slot = jnp.where(position < cap, ids * capp + position, -1)
    table = (slot[:, None] == jnp.arange(slots, dtype=jnp.int32)[None, :]).astype(bf16)

    def pick(values):
        return jnp.sum(table.astype(f32) * values[:, None], axis=0)

    cot_slots = mm(table, cotangent, TN).astype(bf16).reshape(experts, capp, width)

    inputs = tokens.astype(f32)
    g1 = gain_first.astype(f32)
    s1 = lax.rsqrt(jnp.mean(inputs * inputs, axis=-1, keepdims=True) + eps_norm)
    normed_low = (inputs * s1 * g1).astype(bf16)
    q = mm(normed_low, w_query).astype(bf16)
    k = mm(normed_low, w_key).astype(bf16)
    v = mm(normed_low, w_value).astype(bf16)
    near_hot = jnp.asarray(hot_of(np.arange(512) - 256), f32)
    gvec = jnp.einsum("ub,bh->hu", near_hot, bias_table.astype(f32), precision=lax.Precision.HIGHEST)
    attended, probs_low, cot_rows = attn_fwd(gvec.reshape(heads // 2, 2, 512), q, k, v, cot_slots)
    after_attn = inputs + mm(attended, w_output)
    g2 = gain_second.astype(f32)
    s2 = lax.rsqrt(jnp.mean(after_attn * after_attn, axis=-1, keepdims=True) + eps_norm)
    routed_low = (after_attn * s2 * g2).astype(bf16)
    rows = mm(table, routed_low, TN).astype(bf16).reshape(experts, capp, width)
    router_probs = jax.nn.softmax(mm(routed_low, w_router), axis=-1)
    gate = jnp.sum(router_probs * hot32, axis=1)
    gates = jnp.broadcast_to(jnp.pad(pick(gate).reshape(experts, 1, capp), ((0, 0), (0, 0), (0, 128 - capp))), (experts, 8, 128))
    back_tokens, gate_grads, produced, gin_own, gin_oth, gout_own, gout_oth = expert_pass(
        rows, gates, cot_rows, expert_in[0], expert_out[0]
    )
    back_tokens = back_tokens.reshape(slots, width)
    gate_grad_back = gate_grads[:, 0, :capp].reshape(slots)
    around = [(0, 1), (1, 0)]
    gin_oth = lax.ppermute(gin_oth, "dp", around)
    gout_oth = lax.ppermute(gout_oth, "dp", around)

    upstream = cotangent.astype(f32)
    gate_grad = jnp.sum(table.astype(f32) * gate_grad_back[None, :], axis=1)
    logit_grad_low = ((gate_grad * gate)[:, None] * (hot32 - router_probs)).astype(bf16)
    routed_grad = gate[:, None] * mm(table, back_tokens) + mm(logit_grad_low, w_router, NT)
    gdy = g2 * routed_grad
    after_grad = upstream + s2 * gdy - after_attn * (s2 * s2 * s2 * jnp.mean(gdy * after_attn, axis=-1, keepdims=True))
    gain_two = jnp.sum(routed_grad * after_attn * s2, axis=0)
    branch_low = after_grad.astype(bf16)
    attended_grad = mm(branch_low, w_output, NT).astype(bf16)
    grad_router = mm(routed_low, logit_grad_low, TN)
    near, far, dw, normed_grad, returned = attn_bwd(
        q, k, v, attended, attended_grad, probs_low, normed_low, branch_low, w_query, w_key, w_value, produced
    )
    near_index = hot_of((np.arange(512)[None, :] + 128) % 512 - 256 - np.arange(8)[:, None]).reshape(4096, 32)
    far = far.reshape(heads, 8, 2, 128).sum((1, 3))
    table_grad = jnp.einsum("hk,kb->bh", near.reshape(heads, 4096), jnp.asarray(near_index), precision=lax.Precision.HIGHEST)
    table_grad = table_grad.at[15].add(far[:, 0]).at[31].add(far[:, 1])

    gdy = g1 * normed_grad
    input_grad = after_grad + s1 * gdy - inputs * (s1 * s1 * s1 * jnp.mean(gdy * inputs, axis=-1, keepdims=True))
    gain_one = jnp.sum(normed_grad * inputs * s1, axis=0)
    devices = dp_count * experts
    small = [gain_one, gain_two, table_grad.reshape(-1), grad_router.reshape(-1)]
    marks = np.cumsum([0] + [part.size for part in small])
    small = jnp.pad(jnp.concatenate(small), (0, devices * 1024 - int(marks[-1])))
    chunks = 3
    main = dw.reshape(chunks, devices, 4 * width * width // (128 * devices * chunks), 128)
    grad_query, grad_key, grad_value, grad_output, small = reduce_all(main, small.reshape(devices, 8, 128), width)
    small = small.reshape(-1)
    gain_one, gain_two, table_grad, grad_router = (small[marks[i]:marks[i + 1]] for i in range(4))
    combined = mm(table, returned.reshape(slots, width))
    output = (after_attn + gate[:, None] * combined).astype(bf16)
    gin_oth, gout_oth, _ = lax.optimization_barrier((gin_oth, gout_oth, gain_one))
    grad_in = (gin_own + gin_oth.astype(f32))[None]
    grad_out = (gout_own + gout_oth.astype(f32))[None]
    return (
        output,
        input_grad,
        gain_one,
        grad_query,
        grad_key,
        grad_value,
        grad_output,
        table_grad.reshape(bias_table.shape),
        gain_two,
        grad_router.reshape(w_router.shape),
        grad_in,
        grad_out,
    )


def solution(mesh):
    split, whole = P(("dp", "expert"), None), P()
    in_specs = (split, split, split, whole, whole, whole, whole, whole, whole, whole, whole, P("expert", None, None), P("expert", None, None))
    out_specs = (split, split) + (whole,) * 8 + (P("expert", None, "dp"), P("expert", "dp", None))
    return jax.shard_map(
        functools.partial(local, mesh.shape["dp"]), mesh=mesh, in_specs=in_specs, out_specs=out_specs, check_vma=False
    )
```

time: 837 us -> 379 us (0.45)
  matrix products: 333 us -> 34.6 us
  Pallas kernels: 0 us -> 283 us
  waiting for transfers between devices: 150 us -> 0.01 us
  local copies, waits for them, and re-layouts: 141 us -> 25.3 us
  other arithmetic: 98.4 us -> 25.4 us
  blocking collectives: 48 us -> 0 us
  starting transfers between devices: 40.5 us -> 2.09 us
  between operations: 16.6 us -> 1.73 us
    dot_general x41 -> x15, matrix products: 333 us -> 34.6 us  [the longest x13 32.9 us: mm(): return lax.dot_general(a, b, dims, preferred_element_type=jnp.float32)]
    pallas_call x0 -> x4, Pallas kernels: none -> 283 us  [the longest x1 95.8 us: expert_pass(): pl.pallas_call(functools.partial(expert_kernel, groups, tile), in_specs=[...]
    all_to_all x4 -> x0, waiting for transfers between devices: 102 us -> none  [the longest x1 30.5 us: local(): lax.all_to_all(slot_rows, 'expert', split_axis=0, concat_axis=1, tiled=True)]
    dot_general x2 -> x0, local copies, waits for them, and re-layouts: 60.8 us -> none  [score_block(): jnp.einsum('qkb,bh->hqk', onehot, bias_table, preferred_element_type=jnp....]
    convert_element_type x8 -> x6, other arithmetic: 54.8 us -> 3.03 us  [the longest x1 0.83 us: local(): g2 = gain_second.astype(f32)]
    psum x1 -> x0, waiting for transfers between devices: 48.2 us -> none  [local(): lax.psum((gain_one_grad, grad_query_w, grad_key_w, grad_value_w, grad_out...]
    psum x1 -> x0, blocking collectives: 48 us -> none  [local(): lax.psum((gain_one_grad, grad_query_w, grad_key_w, grad_value_w, grad_out...]
    convert_element_type x2 -> x0, local copies, waits for them, and re-layouts: 46.5 us -> none  [local(): score_grad_low = (attn_probs * (prob_grad - row_dot)).astype(jnp.bfloat16)]
  transfers between devices with their start and end apart: 7 -> 2, of which waited for: 5 -> 0; matrix products, arithmetic and copies ran while one was open for 39% -> 10% of each run, Pallas kernels for 0% -> 39%
where the time goes in v1:
time: 379 us; the launch traced here: 372 us
  Pallas kernels  283 us (75%)
  matrix products  34.6 us (9%)
  other arithmetic  25.4 us (7%)
  local copies, waits for them, and re-layouts  25.3 us (7%)
    pallas_call x1, Pallas kernels, expert_pass(): pl.pallas_call(functools.partial(expert_kernel, groups, tile), in_specs=[...  95.8 us
    pallas_call x1, Pallas kernels, reduce_all(): pl.pallas_call(reduce_kernel, in_specs=[vm, vm], out_specs=[vm] * 5, out_...  86.1 us
    pallas_call x1, Pallas kernels, attn_bwd(): pl.pallas_call(functools.partial(bwd_kernel, rows), grid=(pairs,), in_spe...  58.2 us
    pallas_call x1, Pallas kernels, attn_fwd(): pl.pallas_call(functools.partial(fwd_kernel, rows), grid=(pairs,), in_spe...  42.6 us
    dot_general x13, matrix products, mm(): return lax.dot_general(a, b, dims, preferred_element_type=jnp.float32)  32.9 us
    unnamed x90, local copies, waits for them, and re-layouts  18.5 us
  transfers between devices with their start and end apart: 2, of which 0 were waited for; matrix products, arithmetic and copies ran while one was open for 10% of the time, Pallas kernels for 39%

profile of v1, /device:TPU:0, one launch (start us, length us, event | category | flops | bytes accessed | tf_op | source)
XLA Modules:
  0.0 371.8 jit_solution(9080280184558747735)
XLA Ops:
  2.2 1.8 fusion.10
  4.0 1.3 fusion.22
  8.5 2.5 convolution_convert_fusion.1.v_ref
  11.0 1.4 convolution_convert_fusion.2.k_ref
  12.5 1.4 convolution_convert_fusion.3.q_ref
  14.5 4.1 %fusion.8 = bf16[1280,768]{1,0:T(8,128)(2,1)} fusion(bf16[1024,768]{1,0:T(8,128)(2,1)S(1)} %copy-done.21, s32[1024]{0:T(1024)S(1)} %bitcast.69), kind=kOutput, calls=%fused_computation.20 | convolution fusion | flops 2015559680 | bytes 3543040 | tf_op jit(solution)/shard_map/dot_general | solution.py:17
  18.6 42.6 %attn_fwd.1 = (bf16[1024,768]{1,0:T(8,128)(2,1)S(1)}, bf16[12,1024,1024]{2,1,0:T(8,128)(2,1)}, bf16[16,80,768]{2,1,0:T(8,128)(2,1)}) custom-call(f32[6,2,512]{2,1,0:T(2,128)S(1)} %reshape.200.g_ref, bf16[1024,768]{1,0:T(8,128)(2,1)S(1)} %convolution_convert_fusion.3.q_ref, bf16[1024,768]{1,0:T(8,128)(2,1)S(1)} %convolution_convert_fusion.2.k_ref, ...), custom_call_target="tpu_custom_call" | custom-call | tf_op jit(solution)/shard_map/attn_fwd/pallas_call | solution.py:273
  61.2 1.5 multiply_reduce_fusion.2
  63.1 4.2 %fusion.9 = bf16[1280,768]{1,0:T(8,128)(2,1)} fusion(bf16[1024,768]{1,0:T(8,128)(2,1)S(1)} %multiply_convert_fusion, s32[1024]{0:T(1024)S(1)} %bitcast.70), kind=kOutput, calls=%fused_computation.21 | convolution fusion | flops 2015559680 | bytes 3543040 | tf_op jit(solution)/shard_map/dot_general | solution.py:17
  69.5 95.8 %experts.1 = (bf16[16,80,768]{2,1,0:T(8,128)(2,1)}, f32[16,8,128]{2,1,0:T(8,128)}, bf16[16,80,768]{2,1,0:T(8,128)(2,1)}, f32[768,1536]{1,0:T(8,128)}, bf16[768,1...) custom-call(bf16[16,80,768]{2,1,0:T(8,128)(2,1)} %bitcast.60, ...), custom_call_target="tpu_custom_call" | custom-call | tf_op jit(solution)/shard_map/experts/pallas_call | solution.py:180
  165.3 1.6 collective-permute-start
  169.4 2.0 fusion.35
  171.6 4.1 %fusion.3 = f32[1024,768]{1,0:T(8,128)S(1)} fusion(bf16[1280,768]{1,0:T(8,128)(2,1)} %bitcast.76, s32[1024]{0:T(1024)S(1)} %bitcast.73), kind=kOutput, calls=%fused_computation.12 | convolution fusion | flops 2014576640 | bytes 5115904 | tf_op jit(solution)/shard_map/dot_general | solution.py:17
  175.8 1.4 multiply_reduce_fusion
  178.8 2.6 convolution_convert_fusion.d_ref
  181.4 58.2 %attn_bwd.1 = (f32[6,16,512]{2,1,0:T(8,128)}, f32[6,16,256]{2,1,0:T(8,128)}, bf16[6,4,768,128]{3,2,1,0:T(8,128)(2,1)}, f32[1024,768]{1,0:T(8,128)}, bf16[16,80,768]{2,1,0:T(8,128)(2,1)}) custom-call(bf16[1024,768]{1,0:T(8,128)(2,1)} %copy-done.3, bf16[1024,768]{1,0:T(8,128)(2,1)} %copy-done.2, bf16[1024,768]{1,0:T(8,128)(2,1)} %convolution_convert_fusion.1.v_ref, ...), custom_call_target="tpu_custom_call" | custom-call | tf_op jit(solution)/shard_map/attn_bwd/pallas_call | solution.py:394
  242.8 3.8 %fusion.16 = (f32[768]{0:T(1024)S(1)}, f32[1024]{0:T(1024)}) fusion(f32[1024,768]{1,0:T(8,128)} %get-tuple-element.65, bf16[1024,768]{1,0:T(8,128)(2,1)S(1)} %copy-done.18, f32[1024]{0:T(1024)S(1)} %add_rsqrt_fusion.1, f32[768]{0:T(1024)S(1)} %convert_element_type.87), kind=kLoop, calls=%fused_computation.28 | loop fusion | flops 5503232 | bytes 4732928 | tf_op jit(solution)/shard_map/reduce_sum | solution.py:608
  246.6 86.1 %reduce_all.1 = (f32[768,768]{1,0:T(8,128)S(1)}, f32[768,768]{1,0:T(8,128)S(1)}, f32[768,768]{1,0:T(8,128)S(1)}, f32[768,768]{1,0:T(8,128)S(1)}, f32[32,8,128]{2,1,0:T(8,128)S(1)}) custom-call(bf16[3,32,192,128]{3,2,1,0:T(8,128)(2,1)S(1)} %bitcast.51, f32[32,8,128]{2,1,0:T(8,128)S(1)} %fusion.23.small_ref), custom_call_target="tpu_custom_call" | custom-call | tf_op jit(solution)/shard_map/reduce_all/pallas_call | solution.py:515
  332.7 1.4 copy-done.6
  334.1 1.4 copy-done.8
  335.5 1.4 copy-done.10
  337.8 1.4 reshape.214
  339.2 1.4 copy.43
  341.3 1.8 copy.44
  344.4 5.8 %add_convert_fusion = bf16[1024,768]{1,0:T(8,128)(2,1)} fusion(f32[1024,768]{1,0:T(8,128)} %copy-done.12, f32[1024]{0:T(1024)} %copy-done.33, bf16[1280,768]{1,0:T(8,128)(2,1)} %bitcast.75, s32[1024]{0:T(1024)} %bitcast.74), kind=kOutput, calls=%fused_computation.30 | convolution fusion | flops 2016935936 | bytes 6692864 | tf_op jit(solution)/shard_map/dot_general | solution.py:17
  351.1 2.8 fusion.14
  354.0 4.7 %add_bitcast_fusion.1 = f32[1,768,1536]{2,1,0:T(8,128)} fusion(f32[768,1536]{1,0:T(8,128)S(1)} %bitcast.59, bf16[768,1536]{1,0:T(8,128)(2,1)} %collective-permute-done), kind=kLoop, calls=%fused_computation.17 | loop fusion | flops 2359296 | bytes 11796480 | tf_op jit(solution)/shard_map/broadcast_in_dim | solution.py:621
  358.7 4.7 %add_bitcast_fusion = f32[1,1536,768]{2,1,0:T(8,128)} fusion(f32[1536,768]{1,0:T(8,128)S(1)} %bitcast.57, bf16[1536,768]{1,0:T(8,128)(2,1)} %collective-permute-done.1), kind=kLoop, calls=%fused_computation.16 | loop fusion | flops 2359296 | bytes 11796480 | tf_op jit(solution)/shard_map/broadcast_in_dim | solution.py:622
  363.5 1.4 copy.53
  364.9 1.4 copy.54
  367.4 1.4 copy.55
  369.9 1.4 copy.56
  (125 shorter events, 21.2 us)
Async XLA Ops:
  0.6 60.5 %copy-start = (bf16[768,768]{1,0:T(8,128)(2,1)S(1)}, bf16[768,768]{1,0:T(8,128)(2,1)}, u32[]{:S(2)}) copy-start(bf16[768,768]{1,0:T(8,128)(2,1)} %param.26) | copy-start | bytes 3538948
  0.7 6.6 %copy-start.17 = (bf16[1024,768]{1,0:T(8,128)(2,1)S(1)}, bf16[1024,768]{1,0:T(8,128)(2,1)}, u32[]{:S(2)}) copy-start(bf16[1024,768]{1,0:T(8,128)(2,1)} %param.19) | copy-start | bytes 4718596
  4.0 7.1 %copy-start.34 = (f32[1024]{0:T(1024)}, f32[1024]{0:T(1024)S(1)}, u32[]{:S(2)}) copy-start(f32[1024]{0:T(1024)S(1)} %fusion.10) | copy-start | bytes 12292
  6.0 165.6 %copy-start.37 = (s32[1024,1]{0,1:T(1,128)}, s32[1024,1]{0,1:T(1,128)S(1)}, u32[]{:S(2)}) copy-start(s32[1024,1]{0,1:T(1,128)S(1)} %compare_select_fusion) | copy-start | bytes 12292
  8.5 3.9 %copy-start.26 = (bf16[1024,768]{1,0:T(8,128)(2,1)}, bf16[1024,768]{1,0:T(8,128)(2,1)S(1)}, u32[]{:S(2)}) copy-start(bf16[1024,768]{1,0:T(8,128)(2,1)S(1)} %fusion.12.x_ref) | copy-start | bytes 4718596
  8.5 2.5 copy-start.28
  12.5 6.1 %copy-start.2 = (bf16[1024,768]{1,0:T(8,128)(2,1)}, bf16[1024,768]{1,0:T(8,128)(2,1)S(1)}, u32[]{:S(2)}) copy-start(bf16[1024,768]{1,0:T(8,128)(2,1)S(1)} %convolution_convert_fusion.2.k_ref) | copy-start | bytes 4718596
  13.9 4.7 %copy-start.3 = (bf16[1024,768]{1,0:T(8,128)(2,1)}, bf16[1024,768]{1,0:T(8,128)(2,1)S(1)}, u32[]{:S(2)}) copy-start(bf16[1024,768]{1,0:T(8,128)(2,1)S(1)} %convolution_convert_fusion.3.q_ref) | copy-start | bytes 4718596
  62.7 4.6 %copy-start.12 = (f32[1024,768]{1,0:T(8,128)}, f32[1024,768]{1,0:T(8,128)S(1)}, u32[]{:S(2)}) copy-start(f32[1024,768]{1,0:T(8,128)S(1)} %get-tuple-element.111) | copy-start | bytes 9437188
  63.1 4.2 %copy-start.24 = (bf16[1024,768]{1,0:T(8,128)(2,1)}, bf16[1024,768]{1,0:T(8,128)(2,1)S(1)}, u32[]{:S(2)}) copy-start(bf16[1024,768]{1,0:T(8,128)(2,1)S(1)} %multiply_convert_fusion) | copy-start | bytes 4718596
  63.1 4.2 %copy-start.31 = (bf16[768,16]{0,1:T(8,128)(2,1)S(1)}, bf16[768,16]{0,1:T(8,128)(2,1)}, u32[]{:S(2)}) copy-start(bf16[768,16]{0,1:T(8,128)(2,1)} %param.29) | copy-start | bytes 73732
  63.1 4.8 %copy-start.32 = (s32[1024,1]{0,1:T(1,128)S(1)}, s32[1024,1]{0,1:T(1,128)}, u32[]{:S(2)}) copy-start(s32[1024,1]{0,1:T(1,128)} %param.20) | copy-start | bytes 12292
  67.9 107.8 %copy-start.33 = (f32[1024]{0:T(1024)}, f32[1024]{0:T(1024)S(1)}, u32[]{:S(2)}) copy-start(f32[1024]{0:T(1024)S(1)} %fusion.24) | copy-start | bytes 12292
  165.3 188.6 %collective-permute-start = (bf16[768,1536]{1,0:T(8,128)(2,1)}, bf16[768,1536]{1,0:T(8,128)(2,1)}, u32[]{:S(2)}, u32[]{:S(2)}) collective-permute-start(bf16[768,1536]{1,0:T(8,128)(2,1)} %get-tuple-element.75), channel_id=1, source_target_pairs={{0,16},{16,0},{1,17},{17,1},{2,18},{18,2},{3,19},{19,3},{4,20},{20... | collective-permute-start | bytes 7077896 | tf_op jit(solution)/shard_map/ppermute | solution.py:585
  166.9 187.0 %collective-permute-start.1 = (bf16[1536,768]{1,0:T(8,128)(2,1)}, bf16[1536,768]{1,0:T(8,128)(2,1)}, u32[]{:S(2)}, u32[]{:S(2)}) collective-permute-start(bf16[1536,768]{1,0:T(8,128)(2,1)} %get-tuple-element.76), channel_id=1, source_target_pairs={{0,16},{16,0},{1,17},{17,1},{2,18},{18,2},{3,19},{19,3},{4,20},{20... | collective-permute-start | bytes 7077896 | tf_op jit(solution)/shard_map/ppermute | solution.py:586
  171.6 4.1 %copy-start.13 = (f32[1024,768]{1,0:T(8,128)S(1)}, f32[1024,768]{1,0:T(8,128)}, u32[]{:S(2)}) copy-start(f32[1024,768]{1,0:T(8,128)} %copy-done.12) | copy-start | bytes 9437188
  178.8 2.6 copy-start.25
  181.4 60.3 %copy-start.30 = (f32[4096,32]{0,1:T(8,128)S(1)}, f32[4096,32]{0,1:T(8,128)}, u32[]{:S(2)}) copy-start(f32[4096,32]{0,1:T(8,128)} %constant.81.clone) | copy-start | bytes 1572868
  181.4 61.3 %copy-start.18 = (bf16[1024,768]{1,0:T(8,128)(2,1)S(1)}, bf16[1024,768]{1,0:T(8,128)(2,1)}, u32[]{:S(2)}) copy-start(bf16[1024,768]{1,0:T(8,128)(2,1)} %param.19) | copy-start | bytes 4718596
  242.7 3.8 %copy-start.5 = (bf16[6,4,768,128]{3,2,1,0:T(8,128)(2,1)S(1)}, bf16[6,4,768,128]{3,2,1,0:T(8,128)(2,1)}, u32[]{:S(2)}) copy-start(bf16[6,4,768,128]{3,2,1,0:T(8,128)(2,1)} %get-tuple-element.66) | copy-start | bytes 14155780
  341.3 8.9 %copy-start.36 = (f32[1024]{0:T(1024)S(1)}, f32[1024]{0:T(1024)}, u32[]{:S(2)}) copy-start(f32[1024]{0:T(1024)} %copy-done.35) | copy-start | bytes 12292
  344.4 5.9 %copy-start.14 = (f32[1024,768]{1,0:T(8,128)S(1)}, f32[1024,768]{1,0:T(8,128)}, u32[]{:S(2)}) copy-start(f32[1024,768]{1,0:T(8,128)} %copy-done.12) | copy-start | bytes 9437188
  344.4 5.9 %copy-start.16 = (f32[1024,768]{1,0:T(8,128)S(1)}, f32[1024,768]{1,0:T(8,128)}, u32[]{:S(2)}) copy-start(f32[1024,768]{1,0:T(8,128)} %copy-done.15) | copy-start | bytes 9437188
  344.4 5.9 %copy-start.19 = (bf16[1024,768]{1,0:T(8,128)(2,1)S(1)}, bf16[1024,768]{1,0:T(8,128)(2,1)}, u32[]{:S(2)}) copy-start(bf16[1024,768]{1,0:T(8,128)(2,1)} %param.19) | copy-start | bytes 4718596
  344.4 6.1 %copy-start.20 = (f32[1024,768]{1,0:T(8,128)S(1)}, f32[1024,768]{1,0:T(8,128)}, u32[]{:S(2)}) copy-start(f32[1024,768]{1,0:T(8,128)} %get-tuple-element.65) | copy-start | bytes 9437188
  344.4 6.7 %copy-start.23 = (bf16[1024,768]{1,0:T(8,128)(2,1)S(1)}, bf16[1024,768]{1,0:T(8,128)(2,1)}, u32[]{:S(2)}) copy-start(bf16[1024,768]{1,0:T(8,128)(2,1)} %param.21) | copy-start | bytes 4718596
  344.4 9.6 %slice-start.2 = ((s8[4718592]{0:T(1024)(128)(4,1)}), s8[4194304]{0:T(1024)(128)(4,1)S(1)}, s32[]{:S(2)}) async-start(s8[4718592]{0:T(1024)(128)(4,1)} %bitcast.58), calls=%async_computation.2 | async-start | bytes 8388608
  351.1 2.9 slice-start.3
  354.0 4.7 %slice-start = ((s8[4718592]{0:T(1024)(128)(4,1)}), s8[4194304]{0:T(1024)(128)(4,1)S(1)}, s32[]{:S(2)}) async-start(s8[4718592]{0:T(1024)(128)(4,1)} %bitcast.56), calls=%async_computation | async-start | bytes 8388608
  354.0 4.7 %slice-start.1 = ((s8[4718592]{0:T(1024)(128)(4,1)}), s8[524288]{0:T(1024)(128)(4,1)S(1)}, s32[]{:S(2)}) async-start(s8[4718592]{0:T(1024)(128)(4,1)} %bitcast.56), calls=%async_computation.1 | async-start | bytes 1048576
  358.7 4.8 %copy-start.11 = (f32[768,768]{1,0:T(8,128)S(1)}, f32[768,768]{1,0:T(8,128)}, u32[]{:S(2)}) copy-start(f32[768,768]{1,0:T(8,128)} %copy-done.10) | copy-start | bytes 7077892
  367.4 3.9 %copy-start.1 = (bf16[768,768]{1,0:T(8,128)(2,1)S(1)}, bf16[768,768]{1,0:T(8,128)(2,1)}, u32[]{:S(2)}) copy-start(bf16[768,768]{1,0:T(8,128)(2,1)} %param.26) | copy-start | bytes 3538948
  (12 other events, 20.2 us)

commit v2 on v1

v2 whole, which is shorter than its diff:
```python
import functools

import jax
import jax.numpy as jnp
import numpy as np
from jax import lax
from jax.experimental import pallas as pl
from jax.experimental.pallas import tpu as pltpu
from jax.sharding import PartitionSpec as P

NT = (((1,), (1,)), ((), ()))
NN = (((1,), (0,)), ((), ()))
TN = (((0,), (0,)), ((), ()))


def mm(a, b, dims=NN):
    return lax.dot_general(a, b, dims, preferred_element_type=jnp.float32)


MESH = pl.DeviceIdType.MESH
gelu_a, gelu_b = 0.7978845608, 0.044715


def enter(axis_size, across=False):
    me, dp = lax.axis_index("expert"), lax.axis_index("dp")
    barrier = pltpu.get_barrier_semaphore()
    for step in range(1, axis_size):
        pl.semaphore_signal(barrier, inc=1, device_id=(dp, me ^ step), device_id_type=MESH)
    if across:
        pl.semaphore_signal(barrier, inc=1, device_id=(1 - dp, me), device_id_type=MESH)
    pl.semaphore_wait(barrier, axis_size if across else axis_size - 1)
    return dp, me


def expert_kernel(
    groups, tile, early,
    xs_ref, gs_ref, cot_ref, far_ref, win_ref, wout_ref,
    back_ref, gg_ref, ret_ref, gin_ref, gout_ref,
    x_scr, c_scr, g_scr, w1, w2, a_scr, p_scr, ag_scr, pg_scr, r_scr, b_scr, e_scr, sq_scr, gin, gout,
    x_send, x_recv, g_send, g_recv, b_send, b_recv, e_send, e_recv, loc, wsem, csem, rsem, osem, f_send, f_recv,
):
    f32, bf16 = jnp.float32, jnp.bfloat16
    n, cap, width = xs_ref.shape
    ff = win_ref.shape[1]
    half = ff // 2
    size = n // groups
    rows = size * cap
    dp, me = enter(n, True)
    mine = pl.multiple_of(dp * half, 128)
    rest = pl.multiple_of((1 - dp) * half, 128)
    weights = [
        pltpu.make_async_copy(win_ref.at[:, pl.ds(mine, half)], w1.at[:, :half], wsem.at[0]),
        pltpu.make_async_copy(win_ref.at[:, pl.ds(rest, half)], w1.at[:, half:], wsem.at[1]),
        pltpu.make_async_copy(wout_ref.at[pl.ds(mine, half), :], w2.at[:half, :], wsem.at[2]),
        pltpu.make_async_copy(wout_ref.at[pl.ds(rest, half), :], w2.at[half:, :], wsem.at[3]),
    ]
    own = [
        pltpu.make_async_copy(xs_ref.at[me], x_scr.at[0, 0], loc.at[0]),
        pltpu.make_async_copy(gs_ref.at[me], g_scr.at[0, 0], loc.at[1]),
    ]
    cots = [
        pltpu.make_async_copy(cot_ref, c_scr.at[0], csem.at[0]),
        pltpu.make_async_copy(far_ref.at[:early], c_scr.at[1, :early], csem.at[1]),
    ]

    def remote(src, dst, send, recv, dev):
        return pltpu.make_async_remote_copy(src, dst, send, recv, device_id=dev, device_id_type=MESH)

    def x_copy(o):
        return remote(xs_ref.at[me ^ o], x_scr.at[0, o], x_send.at[o], x_recv.at[o], (dp, me ^ o))

    def g_copy(o):
        return remote(gs_ref.at[me ^ o], g_scr.at[0, o], g_send.at[o], g_recv.at[o], (dp, me ^ o))

    def b_copy(o):
        return remote(b_scr.at[o], back_ref.at[me], b_send.at[o], b_recv.at[o], (dp, me ^ o))

    def e_copy(o):
        return remote(e_scr.at[o], gg_ref.at[me], e_send.at[o], e_recv.at[o], (dp, me ^ o))

    def r_copy(o):
        return pltpu.make_async_copy(r_scr.at[o], ret_ref.at[o], rsem.at[o])

    over = (1 - dp, me)
    c_over = remote(cot_ref.at[early:], c_scr.at[1, early:], f_send.at[groups], f_recv.at[groups], over)
    g_over = remote(g_scr.at[0], g_scr.at[1], f_send.at[groups + 1], f_recv.at[groups + 1], over)

    def x_over(g):
        span = slice(g * size, (g + 1) * size)
        return remote(x_scr.at[0, span], x_scr.at[1, span], f_send.at[g], f_recv.at[g], over)

    def each(lo, hi, fn):
        if hi - lo <= 4:
            for o in range(lo, hi):
                fn(o)
        else:
            lax.fori_loop(lo, hi, lambda o, c: (fn(o), c)[1], 0)

    for c in own:
        c.start()
    each(1, n, lambda o: g_copy(o).start())
    each(1, n, lambda o: x_copy(o).start())
    c_over.start()
    for c in cots + weights:
        c.start()
    sq_scr[...] = jnp.zeros_like(sq_scr)

    def gated(side, lo, hi):
        def one(o):
            col = jnp.broadcast_to(g_scr[side, o][:1, :], (128, 128)).T[:cap, :1]
            c_scr[side, o] = (c_scr[side, o].astype(f32) * col).astype(bf16)

        each(lo, hi, one)

    def hidden(x, ct, f):
        u = mm(x, w1[:, f:f + tile])
        back = mm(ct, w2[f:f + tile, :], NT)
        uu = u * u
        t = jnp.tanh(u * (gelu_a + (gelu_a * gelu_b) * uu))
        hp = 0.5 + 0.5 * t
        act = u * hp
        slope = hp + act * ((1.0 - t) * (gelu_a + (3.0 * gelu_a * gelu_b) * uu))
        return act.astype(bf16), (back * slope).astype(bf16)

    for g in range(groups):
        lo, hi = g * size, (g + 1) * size
        if g == 0:
            for c in own + cots[:1]:
                c.wait()
        each(max(lo, 1), hi, lambda o: g_copy(o).wait_recv())
        raw = c_scr[0, lo:hi].reshape(rows, width)
        gated(0, lo, hi)
        each(max(lo, 1), hi, lambda o: x_copy(o).wait_recv())
        x_over(g).start()
        if g == 0:
            for c in weights:
                c.wait()
        x = x_scr[0, lo:hi].reshape(rows, width)
        ct = c_scr[0, lo:hi].reshape(rows, width)
        span = slice(g * rows, (g + 1) * rows)
        for f in range(0, ff, tile):
            act, pre = hidden(x, ct, f)
            if f < half:
                a_scr[span, f:f + tile] = act
                p_scr[span, f:f + tile] = pre
            else:
                ag_scr[:, f - half:f - half + tile] = act
                pg_scr[:, f - half:f - half + tile] = pre
        back = mm(p_scr[span, :], w1[:, :half], NT) + mm(pg_scr[...], w1[:, half:], NT)
        b_scr[lo:hi] = back.astype(bf16).reshape(size, cap, width)
        each(max(lo, 1), hi, lambda o: b_copy(o).start())
        r = mm(a_scr[span, :], w2[:half, :]) + mm(ag_scr[...], w2[half:, :])
        r_scr[lo:hi] = r.astype(bf16).reshape(size, cap, width)
        dots = r * raw.astype(f32)
        part = dots[:, :128]
        for j in range(1, width // 128):
            part = part + dots[:, j * 128:(j + 1) * 128]
        part = part.reshape(size, cap, 128)
        for o in range(lo, hi):
            sq_scr[:cap, :] = part[o - lo]
            line = jnp.sum(sq_scr[...].T, axis=0, keepdims=True)
            e_scr[o] = jnp.broadcast_to(line, (8, 128))
        each(max(lo, 1), hi, lambda o: e_copy(o).start())
    g_over.start()
    each(0, n, lambda o: r_copy(o).start())
    own_back = [
        pltpu.make_async_copy(b_scr.at[0], back_ref.at[me], loc.at[0]),
        pltpu.make_async_copy(e_scr.at[0], gg_ref.at[me], loc.at[1]),
    ]
    for c in own_back:
        c.start()
    total = n * cap

    def gradients(side, first):
        x = x_scr[side].reshape(total, width)
        ct = c_scr[side].reshape(total, width)
        for f in range(0, half, tile):
            part = lax.dot_general(x, p_scr[:, f:f + tile], TN, preferred_element_type=f32)
            if first:
                gin[:, f:f + tile] = part
            else:
                w1[:, f:f + tile] = (gin[:, f:f + tile] + part).astype(bf16)
            part = lax.dot_general(a_scr[:, f:f + tile], ct, TN, preferred_element_type=f32)
            if first:
                gout[f:f + tile, :] = part
            else:
                w2[f:f + tile, :] = (gout[f:f + tile, :] + part).astype(bf16)
                for c in outs(f):
                    c.start()

    def outs(f):
        i = f // tile
        return [
            pltpu.make_async_copy(w1.at[:, f:f + tile], gin_ref.at[:, f:f + tile], osem.at[2 * i]),
            pltpu.make_async_copy(w2.at[f:f + tile, :], gout_ref.at[f:f + tile, :], osem.at[2 * i + 1]),
        ]

    gradients(0, True)
    cots[1].wait()
    c_over.wait()
    g_over.wait()
    gated(1, 0, n)
    for g in range(groups):
        lo, hi = g * size, (g + 1) * size
        x_over(g).wait()
        x = x_scr[1, lo:hi].reshape(rows, width)
        ct = c_scr[1, lo:hi].reshape(rows, width)
        for f in range(0, half, tile):
            act, pre = hidden(x, ct, f)
            a_scr[g * rows:(g + 1) * rows, f:f + tile] = act
            p_scr[g * rows:(g + 1) * rows, f:f + tile] = pre
    gradients(1, False)
    for f in range(0, half, tile):
        for c in outs(f):
            c.wait()
    for c in own_back:
        c.wait()
    each(0, n, lambda o: r_copy(o).wait())
    each(1, n, lambda o: x_copy(o).wait_send())
    each(1, n, lambda o: g_copy(o).wait_send())
    each(1, n, lambda o: b_copy(o).wait())
    each(1, n, lambda o: e_copy(o).wait())


def expert_pass(xs, gs, cot, far, w_in, w_out):
    f32, bf16 = jnp.float32, jnp.bfloat16
    n, cap, width = xs.shape
    ff = w_in.shape[1]
    half = ff // 2
    groups, tile = (4, 512) if n * cap <= 1280 else (8, 256)
    rows = n // groups * cap
    hbm = pl.BlockSpec(memory_space=pl.ANY)
    dma = pltpu.SemaphoreType.DMA
    flat = jax.ShapeDtypeStruct((n, cap, width), bf16)
    return pl.pallas_call(
        functools.partial(expert_kernel, groups, tile, n // 2),
        in_specs=[hbm] * 6,
        out_specs=[hbm] * 5,
        out_shape=[
            flat, jax.ShapeDtypeStruct((n, 8, 128), f32), flat,
            jax.ShapeDtypeStruct((width, half), bf16), jax.ShapeDtypeStruct((half, width), bf16),
        ],
        scratch_shapes=[
            pltpu.VMEM((2, n, cap, width), bf16), pltpu.VMEM((2, n, cap, width), bf16), pltpu.VMEM((2, n, 8, 128), f32),
            pltpu.VMEM((width, ff), bf16), pltpu.VMEM((ff, width), bf16),
            pltpu.VMEM((n * cap, half), bf16), pltpu.VMEM((n * cap, half), bf16),
            pltpu.VMEM((rows, half), bf16), pltpu.VMEM((rows, half), bf16),
            pltpu.VMEM((n, cap, width), bf16), pltpu.VMEM((n, cap, width), bf16), pltpu.VMEM((n, 8, 128), f32),
            pltpu.VMEM((128, 128), f32), pltpu.VMEM((width, half), f32), pltpu.VMEM((half, width), f32),
        ] + [dma((n,))] * 8 + [dma((2,)), dma((4,)), dma((2,)), dma((n,)), dma((2 * half // tile,)), dma((groups + 2,)), dma((groups + 2,))],
        compiler_params=pltpu.CompilerParams(collective_id=1, has_side_effects=True, vmem_limit_bytes=62 << 20),
        name="experts",
    )(xs, gs, cot, far, w_in, w_out)

def fwd_kernel(rows, g_ref, q_ref, k_ref, v_ref, cs_ref, o_ref, p_ref, cr_ref, cp_ref, b_scr, send, recv, loc, f_send, f_recv):
    seq = q_ref.shape[0]
    blocks = seq // 128
    step = pl.program_id(0)

    n = cs_ref.shape[0]
    me, dp = lax.axis_index("expert"), lax.axis_index("dp")
    quarter = n // 4

    def c_copy(o):
        return pltpu.make_async_remote_copy(
            cs_ref.at[me ^ o], cr_ref.at[o], send.at[o], recv.at[o], device_id=(dp, me ^ o), device_id_type=MESH
        )

    def over(i):
        span = pl.ds(i * quarter, quarter)
        return pltpu.make_async_remote_copy(
            cr_ref.at[span], cp_ref.at[span], f_send.at[i], f_recv.at[i], device_id=(1 - dp, me), device_id_type=MESH
        )

    home = pltpu.make_async_copy(cs_ref.at[me], cr_ref.at[0], loc.at[0])

    @pl.when(step == 0)
    def _():
        enter(n, True)
        home.start()
        for o in range(1, n):
            c_copy(o).start()

    for i in range(2):

        @pl.when(step == 2 + 2 * i)
        def _():
            if i == 0:
                home.wait()
            for o in range(max(1, i * quarter), (i + 1) * quarter):
                c_copy(o).wait_recv()
            over(i).start()

    lane = lax.broadcasted_iota(jnp.int32, (rows, 128), 1)
    for hh in range(2):
        own = (lane >= 64) if hh else (lane < 64)
        g = g_ref[0, hh:hh + 1, :]
        near = pltpu.roll(jnp.broadcast_to(g, (128, 512)), 384, axis=1, stride=1, stride_axis=0)
        mid = (blocks - 2) * 128
        b_scr[:, :mid] = jnp.broadcast_to(g[:, :1], (128, mid))
        b_scr[:, mid:mid + 384] = near[:, :384]
        b_scr[:, mid + 384:] = jnp.broadcast_to(g[:, 511:], (128, b_scr.shape[1] - mid - 384))
        for i in range(seq // rows):
            r0 = i * rows
            q = q_ref[r0:r0 + rows, :]
            qm = jnp.where(own, q * jnp.bfloat16(0.125), jnp.bfloat16(0))
            s = mm(qm, k_ref[...], NT)
            parts = []
            for a in range(rows // 128):
                c0 = (blocks - 1 - (r0 // 128 + a)) * 128
                parts.append(s[a * 128:(a + 1) * 128] + b_scr[:, c0:c0 + seq])
            s = jnp.concatenate(parts, 0) if len(parts) > 1 else parts[0]
            m = jnp.max(s, axis=-1, keepdims=True)
            e = jnp.exp(s - m)
            inv = 1.0 / jnp.sum(e, axis=-1, keepdims=True)
            p = (e * inv).astype(jnp.bfloat16)
            p_ref[hh, r0:r0 + rows, :] = p
            o = mm(p, v_ref[...]).astype(jnp.bfloat16)
            if hh == 0:
                o_ref[r0:r0 + rows, :] = o
            else:
                o_ref[r0:r0 + rows, :] = jnp.where(own, o, o_ref[r0:r0 + rows, :])

    @pl.when(step == pl.num_programs(0) - 1)
    def _():
        for o in range(1, n):
            c_copy(o).wait_send()
        for o in range(n // 2, n):
            c_copy(o).wait_recv()
        for i in range(2):
            over(i).wait()


def attn_fwd(gvec, q, k, v, cs, rows=256):
    seq, width = q.shape
    pairs = width // 128
    n = cs.shape[0]
    col = pl.BlockSpec((seq, 128), lambda h: (0, h))
    hbm = pl.BlockSpec(memory_space=pl.ANY)
    dma = pltpu.SemaphoreType.DMA
    return pl.pallas_call(
        functools.partial(fwd_kernel, rows),
        grid=(pairs,),
        in_specs=[pl.BlockSpec((1, 2, 512), lambda h: (h, 0, 0)), col, col, col, hbm],
        out_specs=[col, pl.BlockSpec((2, seq, seq), lambda h: (h, 0, 0)), hbm, hbm],
        out_shape=[
            jax.ShapeDtypeStruct((seq, width), jnp.bfloat16),
            jax.ShapeDtypeStruct((2 * pairs, seq, seq), jnp.bfloat16),
            jax.ShapeDtypeStruct(cs.shape, cs.dtype),
            jax.ShapeDtypeStruct((n // 2, *cs.shape[1:]), cs.dtype),
        ],
        scratch_shapes=[pltpu.VMEM((128, 2 * seq - 128), jnp.float32), dma((n,)), dma((n,)), dma((1,)), dma((2,)), dma((2,))],
        compiler_params=pltpu.CompilerParams(
            dimension_semantics=("arbitrary",), collective_id=3, has_side_effects=True, vmem_limit_bytes=48 << 20
        ),
        name="attn_fwd",
    )(gvec, q, k, v, cs)


def bwd_kernel(
    rows, merge, q_ref, k_ref, v_ref, o_ref, p_ref, wq_ref, wk_ref, wv_ref,
    tok_ref, cot_ref, after_ref, stat_ref, probs_ref, g1_ref, g2_ref, wr_ref, wo_ref, back_ref, gg_ref, rs_ref,
    ig_ref, small_out, sum_ref, rr_ref,
    ds_scr, qt_scr, dt_scr, near_scr, far_scr, xt_scr, d_scr, br_scr, dz_scr, nf_scr, ng_scr, rt_scr, gc_scr,
    acc, inbox, done, s_acc, s_inbox, s_done, send, recv, loc, r_send, r_recv, s_send, s_recv, out_sem,
):
    seq = q_ref.shape[0]
    blocks = seq // 128
    step = pl.program_id(0)
    width = tok_ref.shape[1]
    pairs = width // 128
    f32, bf16 = jnp.float32, jnp.bfloat16
    chunks, total, depth, _ = acc.shape
    n = total // 2
    me, dp = lax.axis_index("expert"), lax.axis_index("dp")
    rounds = rounds_of(n)
    count = len(rounds)

    def place(bits):
        rank, devices = 0, []
        for i, bit in enumerate(bits):
            rank = rank + (dp if bit < 0 else (me >> bit) & 1) * (1 << i)
        for mask in range(1, 1 << len(bits)):
            flip = sum(1 << bit for i, bit in enumerate(bits) if bit >= 0 and mask >> i & 1)
            across = any(bit < 0 and mask >> i & 1 for i, bit in enumerate(bits))
            devices.append((1 - dp if across else dp, me ^ flip))
        return rank, devices

    ranks, spans, at, base, size, lead = [place(bits) for bits in rounds], [], 0, 0, total, 0
    for r, bits in enumerate(rounds):
        size //= 1 << len(bits)
        spans.append((at, at + ranks[r][0] * size, size, base, lead))
        at, base, lead = at + ranks[r][0] * size, base + ((1 << len(bits)) - 1) * size, lead + (1 << len(bits)) - 1
    links = lead

    def spread(lane, r):
        mine, box, _, ss, rs, _ = lane
        start, _, size, base, lead = spans[r]
        rank, devices = ranks[r]
        return [
            pltpu.make_async_remote_copy(
                mine.at[pl.ds(start + (rank ^ m) * size, size)], box.at[base + (m - 1) * size:base + m * size],
                ss.at[lead + m - 1], rs.at[lead + m - 1], device_id=devices[m - 1], device_id_type=MESH,
            )
            for m in range(1, len(devices) + 1)
        ]

    def fold(lane, r):
        mine, box, out, _, _, kind = lane
        _, keep, size, base, _ = spans[r]
        here = pl.ds(keep, size)
        part = mine[here].astype(jnp.float32)
        for m in range(len(ranks[r][1])):
            part = part + box[base + m * size:base + (m + 1) * size].astype(jnp.float32)
        (out if r == count - 1 else mine)[here] = part.astype(kind)

    def share(lane, r):
        _, _, out, ss, rs, _ = lane
        _, keep, size, _, lead = spans[r]
        piece = out.at[pl.ds(keep, size)]
        return [
            pltpu.make_async_remote_copy(
                piece, piece, ss.at[links + lead + m - 1], rs.at[links + lead + m - 1], device_id=dev, device_id_type=MESH
            )
            for m, dev in enumerate(ranks[r][1], 1)
        ]

    def event(lane, e):
        if 0 < e <= count:
            for c in spread(lane, e - 1):
                c.wait()
            fold(lane, e - 1)
        elif e > count:
            for c in share(lane, 2 * count - e):
                c.wait()
        if e < count:
            for c in spread(lane, e):
                c.start()
        elif e < 2 * count:
            for c in share(lane, 2 * count - 1 - e):
                c.start()

    last = 2 * count
    gaps = [3] + [6] * (count - 1)
    gaps = gaps + gaps[::-1]
    due = [sum(gaps[:e]) for e in range(last + 1)]

    def lane_of(c):
        return (acc.at[c], inbox.at[c], done.at[c], r_send.at[c], r_recv.at[c], jnp.bfloat16)

    tiny = (s_acc, s_inbox, s_done, s_send, s_recv, jnp.float32)

    def finish(c):
        return pltpu.make_async_copy(done.at[c], sum_ref.at[c], out_sem.at[c])

    def advance(slot):
        for e in range(last, 0, -1):
            if (slot - due[e] - 2) % 3:
                continue
            ready = step + (slot - due[e] - 2) // 3 + 1
            c = ready // merge - 1

            @pl.when((ready >= merge) & (ready % merge == 0))
            def _():
                event(lane_of(c), e)
                if e == last:
                    finish(c).start()

    def r_copy(o):
        return pltpu.make_async_remote_copy(
            rs_ref.at[o], rr_ref.at[me], send.at[o], recv.at[o], device_id=(dp, me ^ o), device_id_type=MESH
        )

    home = pltpu.make_async_copy(rs_ref.at[0], rr_ref.at[me], loc.at[0])
    experts, cap = rs_ref.shape[0], rs_ref.shape[1]

    @pl.when(step == 0)
    def _():
        others = [(dp, me ^ o) for o in range(1, n)]
        for bits, (_, devices) in zip(rounds, ranks):
            if -1 in bits:
                others += [dev for m, dev in enumerate(devices, 1) if m >> bits.index(-1) & 1]
        barrier = pltpu.get_barrier_semaphore()
        for dev in others:
            pl.semaphore_signal(barrier, inc=1, device_id=dev, device_id_type=MESH)
        pl.semaphore_wait(barrier, len(others))
        home.start()
        for o in range(1, n):
            r_copy(o).start()
        s_acc[...] = jnp.zeros_like(s_acc)
        rt_scr[...] = jnp.zeros_like(rt_scr)
        column = lax.broadcasted_iota(jnp.int32, (cap, 128), 1)

        def split(x, _):
            col = jnp.broadcast_to(gg_ref[x][:1, :], (128, 128)).T[:cap, :1]
            high = col.astype(bf16).astype(f32)
            mid = (col - high).astype(bf16).astype(f32)
            low = col - high - mid
            gc_scr[x] = jnp.where(column == 0, high, jnp.where(column == 1, mid, jnp.where(column == 2, low, 0.0))).astype(bf16)
            return 0

        lax.fori_loop(0, experts, split, 0)
        slots = experts * cap
        back = back_ref[...].reshape(slots, width)
        marks = gc_scr[...].reshape(slots, 128)
        where = lax.broadcasted_iota(jnp.int32, (rows, slots), 1)
        choice = lax.broadcasted_iota(jnp.int32, (rows, probs_ref.shape[1]), 1)
        for i in range(0, seq, rows):
            here = slice(i, i + rows)
            s1, s2, gate = stat_ref[here, 0:1], stat_ref[here, 1:2], stat_ref[here, 2:3]
            table = (stat_ref[here, 3:4].astype(jnp.int32) == where).astype(f32).astype(bf16)
            hot = (stat_ref[here, 4:5].astype(jnp.int32) == choice).astype(f32)
            triple = mm(table, marks)
            gate_grad = triple[:, 0:1] + triple[:, 1:2] + triple[:, 2:3]
            lg = ((gate_grad * gate) * (hot - probs_ref[here, :])).astype(bf16)
            rg = mm(table, back) + mm(lg, wr_ref[...], NT)
            gdy = g2_ref[...] * rg
            scaled = after_ref[here, :] * s2
            mean = jnp.sum(gdy * scaled, axis=-1, keepdims=True) * (1.0 / width)
            after = cot_ref[here, :].astype(f32) + s2 * (gdy - scaled * mean)
            routed = (scaled * g2_ref[...]).astype(bf16)
            rt_scr[1:, :] += lax.dot_general(lg, routed, TN, preferred_element_type=f32)
            rt_scr[:1, :] += jnp.sum(rg * scaled, axis=0, keepdims=True)
            ig_ref[here, :] = after
            low = after.astype(bf16)
            br_scr[here, :] = low
            d_scr[here, :] = mm(low, wo_ref[...], NT).astype(bf16)
            xt_scr[:, here] = (tok_ref[here, :].astype(f32) * s1 * g1_ref[...]).astype(bf16).T

    cols = pl.ds(pl.multiple_of(step * 128, 128), 128)
    lane = lax.broadcasted_iota(jnp.int32, (rows, 128), 1)
    sub = lax.broadcasted_iota(jnp.int32, (128, seq), 0)
    qt = q_ref[...].T
    dt = d_scr[:, cols].T
    zero = jnp.bfloat16(0)
    for hh in range(2):
        half = (sub >= 64) if hh else (sub < 64)
        qt_scr[:, hh * seq:(hh + 1) * seq] = jnp.where(half, qt, zero)
        dt_scr[:, hh * seq:(hh + 1) * seq] = jnp.where(half, dt, zero)
    for hh in range(2):
        own = (lane >= 64) if hh else (lane < 64)
        near_scr[...] = jnp.zeros_like(near_scr)
        far_scr[...] = jnp.zeros_like(far_scr)
        for i in range(seq // rows):
            r0 = i * rows
            d = jnp.where(own, d_scr[r0:r0 + rows, cols], zero)
            grown = mm(d, v_ref[...], NT)
            delta = jnp.sum(d.astype(jnp.float32) * o_ref[r0:r0 + rows, :].astype(jnp.float32), axis=-1, keepdims=True)
            ds = p_ref[hh, r0:r0 + rows, :].astype(jnp.float32) * (grown - delta)
            low = ds.astype(jnp.bfloat16)
            ds_scr[r0:r0 + rows, :] = low
            for a in range(rows // 128):
                bi = r0 // 128 + a
                strip = ds[a * 128:(a + 1) * 128]
                lo, hi = max(bi - 1, 0), min(bi + 2, blocks)
                near_scr[:, (lo - bi + 1) * 128:(hi - bi + 1) * 128] += strip[:, lo * 128:hi * 128]
                if lo > 0:
                    t = strip[:, :128]
                    for j in range(1, lo):
                        t = t + strip[:, j * 128:(j + 1) * 128]
                    far_scr[:, :128] += t
                if hi < blocks:
                    t = strip[:, hi * 128:(hi + 1) * 128]
                    for j in range(hi + 1, blocks):
                        t = t + strip[:, j * 128:(j + 1) * 128]
                    far_scr[:, 128:] += t
            dq = (0.125 * mm(low, k_ref[...])).astype(jnp.bfloat16)
            if hh == 0:
                dz_scr[r0:r0 + rows, :128] = dq
            else:
                dz_scr[r0:r0 + rows, :128] = jnp.where(own, dq, dz_scr[r0:r0 + rows, :128])
        part = mm(qt_scr[:, hh * seq:(hh + 1) * seq], ds_scr[...])
        dkt = part if hh == 0 else dkt + part
        a = near_scr[...]
        w = 128
        while w > 1:
            w //= 2
            a = a[:w] + pltpu.roll(a[w:], 512 - w, axis=1)
        nf_scr[pl.ds(2 * step + hh, 1), :512] = a
        nf_scr[pl.ds(2 * step + hh, 1), 512:] = jnp.sum(far_scr[...], axis=0, keepdims=True)
        if hh == 0:
            advance(0)
    advance(1)
    dz_scr[:, 128:256] = (0.125 * dkt).astype(jnp.bfloat16).T
    dvt = mm(dt_scr[...], p_ref[...].reshape(2 * seq, seq))
    dz_scr[:, 256:] = dvt.astype(jnp.bfloat16).T
    dz = dz_scr[...]
    dw = mm(xt_scr[...], dz).astype(jnp.bfloat16)
    go = lax.dot_general(o_ref[...], br_scr[...], TN, preferred_element_type=f32).astype(bf16)
    tiles = [dw[:, j * 128:(j + 1) * 128] for j in range(3)]
    tiles.append(jnp.concatenate([go[:, j * 128:(j + 1) * 128] for j in range(pairs)], axis=0))
    mine = step // merge
    per = width // depth
    for turn in range(merge):

        @pl.when(step % merge == turn)
        def _():
            for j in range(4):
                at = (turn * 4 + j) * per
                acc[mine, at:at + per] = tiles[j].reshape(per, depth, 128)

    w = jnp.concatenate([wq_ref[...], wk_ref[...], wv_ref[...]], axis=1)
    ng = mm(dz, w, NT)

    @pl.when(step == 0)
    def _():
        ng_scr[...] = ng

    @pl.when(step > 0)
    def _():
        ng_scr[...] += ng

    advance(2)

    @pl.when((step + 1) % merge == 0)
    def _():
        event(lane_of(mine), 0)

    @pl.when(step == pairs - 1)
    def _():
        gain = jnp.zeros((1, width), f32)
        for i in range(0, seq, rows):
            here = slice(i, i + rows)
            scaled = tok_ref[here, :].astype(f32) * stat_ref[here, 0:1]
            gain = gain + jnp.sum(ng_scr[here, :] * scaled, axis=0, keepdims=True)
        pieces = [gain] + [nf_scr[h:h + 1, :] for h in range(2 * pairs)] + [rt_scr[h:h + 1, :] for h in range(rt_scr.shape[0])]
        for i, piece in enumerate(pieces):
            for j in range(6):
                r = i * 6 + j
                s_acc[r // 8, r % 8:r % 8 + 1, :] = piece[:, j * 128:(j + 1) * 128]
        event(tiny, 0)
        left = []
        for c in range(chunks):
            ready = 3 * (c * merge + merge - 1) + 2
            left.append([e for e in range(1, last + 1) if ready + due[e] > 3 * pairs - 1])
        for turn in range(1, last + 1):
            event(tiny, turn)
            for c in range(chunks):
                if left[c]:
                    e = left[c].pop(0)
                    event(lane_of(c), e)
                    if e == last:
                        finish(c).start()
            if turn == 1:
                for i in range(0, seq, rows):
                    here = slice(i, i + rows)
                    s1 = stat_ref[here, 0:1]
                    scaled = tok_ref[here, :].astype(f32) * s1
                    gdy = g1_ref[...] * ng_scr[here, :]
                    mean = jnp.sum(gdy * scaled, axis=-1, keepdims=True) * (1.0 / width)
                    ig_ref[here, :] += s1 * (gdy - scaled * mean)
        small_out[...] = s_done[...]
        for c in range(chunks):
            finish(c).wait()
        home.wait()
        for o in range(1, n):
            r_copy(o).wait()


def rounds_of(n):
    bits = n.bit_length() - 1
    if bits == 4:
        return [[0], [1, -1], [2, 3]]
    rest = list(range(1, bits)) + [-1]
    return [[0]] + [rest[i:i + 2] for i in range(0, len(rest), 2)]


def attn_bwd(q, k, v, o, p, wq, wk, wv, tokens, cotangent, after_attn, stats, probs, g1, g2, wr, wo, back, gg, rs, rows=256):
    f32, bf16 = jnp.float32, jnp.bfloat16
    seq, width = q.shape
    pairs = width // 128
    n, cap = rs.shape[:2]
    total = 2 * n
    experts = probs.shape[1]
    links = sum((1 << len(bits)) - 1 for bits in rounds_of(n))
    merge = 1
    while 4 * width * merge % (total * 8):
        merge += 1
    chunks = pairs // merge
    depth = 4 * width * merge // total
    col = pl.BlockSpec((seq, 128), lambda h: (0, h))
    wcol = pl.BlockSpec((width, 128), lambda h: (0, h))

    def whole(shape):
        return pl.BlockSpec(shape, lambda h: (0,) * len(shape), pipeline_mode=pl.Buffered(1))

    hbm = pl.BlockSpec(memory_space=pl.ANY)
    dma = pltpu.SemaphoreType.DMA
    small = (total, 8, 128)
    store = pltpu.VMEM((chunks, total, depth, 128), bf16)
    small_store = pltpu.VMEM(small, f32)
    singles = (tokens, cotangent, after_attn, stats, probs, g1, g2, wr, wo, back, gg)
    return pl.pallas_call(
        functools.partial(bwd_kernel, rows, merge),
        grid=(pairs,),
        in_specs=[col] * 4 + [pl.BlockSpec((2, seq, seq), lambda h: (h, 0, 0))] + [wcol] * 3 + [whole(x.shape) for x in singles] + [hbm],
        out_specs=[whole((seq, width)), whole(small), hbm, hbm],
        out_shape=[
            jax.ShapeDtypeStruct((seq, width), f32),
            jax.ShapeDtypeStruct(small, f32),
            jax.ShapeDtypeStruct((chunks, total, depth, 128), bf16),
            jax.ShapeDtypeStruct(rs.shape, rs.dtype),
        ],
        scratch_shapes=[
            pltpu.VMEM((seq, seq), bf16), pltpu.VMEM((128, 2 * seq), bf16), pltpu.VMEM((128, 2 * seq), bf16),
            pltpu.VMEM((128, 512), f32), pltpu.VMEM((128, 256), f32),
            pltpu.VMEM((width, seq), bf16), pltpu.VMEM((seq, width), bf16), pltpu.VMEM((seq, width), bf16), pltpu.VMEM((seq, 384), bf16),
            pltpu.VMEM((2 * pairs + 4, 768), f32), pltpu.VMEM((seq, width), f32), pltpu.VMEM((1 + experts, width), f32),
            pltpu.VMEM((n, cap, 128), bf16),
            store, store, store, small_store, small_store, small_store,
            dma((n,)), dma((n,)), dma((1,)),
            dma((chunks, 2 * links)), dma((chunks, 2 * links)), dma((2 * links,)), dma((2 * links,)), dma((chunks,)),
        ],
        compiler_params=pltpu.CompilerParams(
            dimension_semantics=("arbitrary",), collective_id=4, has_side_effects=True, vmem_limit_bytes=63 << 20
        ),
        name="attn_bwd",
    )(q, k, v, o, p, wq, wk, wv, *singles, rs)

def finish_kernel(sum_ref, q_ref, k_ref, v_ref, o_ref):
    for j, out in enumerate((q_ref, k_ref, v_ref)):
        out[...] = sum_ref[0, j].astype(jnp.float32)
    for i in range(sum_ref.shape[2] // 128):
        o_ref[:, i * 128:(i + 1) * 128] = sum_ref[0, 3, i * 128:(i + 1) * 128].astype(jnp.float32)


def finish_sums(sums):
    pairs, _, depth, _ = sums.shape
    col = pl.BlockSpec((depth, 128), lambda h: (0, h))
    return pl.pallas_call(
        finish_kernel,
        grid=(pairs,),
        in_specs=[pl.BlockSpec((1, 4, depth, 128), lambda h: (h, 0, 0, 0))],
        out_specs=[col] * 3 + [pl.BlockSpec((128, depth), lambda h: (h, 0))],
        out_shape=[jax.ShapeDtypeStruct((depth, 128 * pairs), jnp.float32)] * 4,
        compiler_params=pltpu.CompilerParams(dimension_semantics=("arbitrary",), vmem_limit_bytes=16 << 20),
        name="finish_sums",
    )(sums)

eps_norm = 1e-06
thresholds = (12, 16, 23, 32, 46, 64, 91)


def bucket_of(offset):
    distance = np.abs(offset)
    far = 8 + sum((distance >= t).astype(np.int32) for t in thresholds)
    return np.where(distance < 8, distance, far) + 16 * (offset > 0)


def hot_of(offset):
    return (bucket_of(offset)[..., None] == np.arange(32)).astype(np.float32)


def local(dp_count, tokens, routes, cotangent, gain_first, w_query, w_key, w_value, w_output, bias_table, gain_second, w_router, expert_in, expert_out):
    f32, bf16 = jnp.float32, jnp.bfloat16
    seq, width = tokens.shape
    heads = bias_table.shape[1]
    experts = w_router.shape[1]
    cap = (5 * seq + 4 * experts - 1) // (4 * experts)
    capp = (cap + 15) // 16 * 16
    slots = experts * capp
    ids = routes[:, 0]
    hot = (ids[:, None] == jnp.arange(experts, dtype=jnp.int32)[None, :]).astype(bf16)
    order = jnp.arange(seq, dtype=jnp.int32)
    before = (order[:, None] > order[None, :]).astype(bf16)
    hot32 = hot.astype(f32)
    position = jnp.sum(mm(before, hot) * hot32, axis=1).astype(jnp.int32)
    slot = jnp.where(position < cap, ids * capp + position, -1)
    table = (slot[:, None] == jnp.arange(slots, dtype=jnp.int32)[None, :]).astype(bf16)

    def pick(values):
        return jnp.sum(table.astype(f32) * values[:, None], axis=0)

    cot_slots = mm(table, cotangent, TN).astype(bf16).reshape(experts, capp, width)

    inputs = tokens.astype(f32)
    g1 = gain_first.astype(f32)
    s1 = lax.rsqrt(jnp.mean(inputs * inputs, axis=-1, keepdims=True) + eps_norm)
    normed_low = (inputs * s1 * g1).astype(bf16)
    q = mm(normed_low, w_query).astype(bf16)
    k = mm(normed_low, w_key).astype(bf16)
    v = mm(normed_low, w_value).astype(bf16)
    near_hot = jnp.asarray(hot_of(np.arange(512) - 256), f32)
    gvec = jnp.einsum("ub,bh->hu", near_hot, bias_table.astype(f32), precision=lax.Precision.HIGHEST)
    attended, probs_low, cot_rows, cot_far = attn_fwd(gvec.reshape(heads // 2, 2, 512), q, k, v, cot_slots)
    after_attn = inputs + mm(attended, w_output)
    g2 = gain_second.astype(f32)
    s2 = lax.rsqrt(jnp.mean(after_attn * after_attn, axis=-1, keepdims=True) + eps_norm)
    routed_low = (after_attn * s2 * g2).astype(bf16)
    rows = mm(table, routed_low, TN).astype(bf16).reshape(experts, capp, width)
    router_probs = jax.nn.softmax(mm(routed_low, w_router), axis=-1)
    gate = jnp.sum(router_probs * hot32, axis=1)
    gates = jnp.broadcast_to(jnp.pad(pick(gate).reshape(experts, 1, capp), ((0, 0), (0, 0), (0, 128 - capp))), (experts, 8, 128))
    back_tokens, gate_grads, produced, grad_in, grad_out = expert_pass(rows, gates, cot_rows, cot_far, expert_in[0], expert_out[0])
    stats = jnp.stack([s1[:, 0], s2[:, 0], gate, slot.astype(f32), ids.astype(f32), gate, gate, gate], axis=1)
    input_grad, small, sums, returned = attn_bwd(
        q, k, v, attended, probs_low, w_query, w_key, w_value, tokens, cotangent, after_attn, stats, router_probs,
        g1[None, :], g2[None, :], w_router, w_output, back_tokens, gate_grads, produced,
    )
    grad_query, grad_key, grad_value, grad_output = finish_sums(sums.reshape(heads // 2, 4, width, 128))
    small = small.reshape(-1)[:(2 + heads + experts) * 768].reshape(-1, 768)
    gain_one, strips, gain_two, router_rows = small[0], small[1:1 + heads], small[1 + heads], small[2 + heads:]
    grad_router = router_rows.T
    near_index = jnp.asarray(hot_of((np.arange(512) + 128) % 512 - 256))
    table_grad = jnp.einsum("hu,ub->bh", strips[:, :512], near_index, precision=lax.Precision.HIGHEST)
    left, right = jnp.sum(strips[:, 512:640], axis=1), jnp.sum(strips[:, 640:], axis=1)
    bucket = jnp.arange(32, dtype=jnp.int32)[:, None]
    table_grad = table_grad + jnp.where(bucket == 15, left[None, :], 0.0) + jnp.where(bucket == 31, right[None, :], 0.0)
    combined = mm(table, returned.reshape(slots, width))
    output = (after_attn + gate[:, None] * combined).astype(bf16)
    return (
        output,
        input_grad,
        gain_one,
        grad_query,
        grad_key,
        grad_value,
        grad_output,
        table_grad,
        gain_two,
        grad_router,
        grad_in[None].astype(f32),
        grad_out[None].astype(f32),
    )


def solution(mesh):
    split, whole = P(("dp", "expert"), None), P()
    in_specs = (split, split, split, whole, whole, whole, whole, whole, whole, whole, whole, P("expert", None, None), P("expert", None, None))
    out_specs = (split, split) + (whole,) * 8 + (P("expert", None, "dp"), P("expert", "dp", None))
    return jax.shard_map(
        functools.partial(local, mesh.shape["dp"]), mesh=mesh, in_specs=in_specs, out_specs=out_specs, check_vma=False
    )
```

time: 379 us -> 324 us (0.85)
  Pallas kernels: 283 us -> 267 us
  other arithmetic: 25.4 us -> 10.4 us
  local copies, waits for them, and re-layouts: 25.3 us -> 14 us
  matrix products: 34.6 us -> 25.7 us
    pallas_call x3, Pallas kernels: 240 us -> 221 us  [the longest x1 119 us: attn_bwd(): pl.pallas_call(functools.partial(bwd_kernel, rows, merge), grid=(pairs,),...]
    unnamed x90 -> x52, local copies, waits for them, and re-layouts: 18.5 us -> 6.34 us
    broadcast_in_dim x2 -> x0, other arithmetic: 9.44 us -> none  [the longest x1 4.75 us: local(): grad_out = (gout_own + gout_oth.astype(f32))[None]]
    dot_general x13 -> x9, matrix products: 32.9 us -> 24.5 us  [mm(): return lax.dot_general(a, b, dims, preferred_element_type=jnp.float32)]
    reduce_sum x3 -> x1, other arithmetic: 5.81 us -> 0.11 us  [local(): jnp.sum(strips[:, 512:640], axis=1)]
    convert_element_type x3, other arithmetic: 1.51 us -> 5.38 us  [the longest x1 2.82 us: local(): grad_in[None].astype(f32)]
  transfers between devices with their start and end apart: 2 -> 0, of which waited for: 0 -> 0; matrix products, arithmetic and copies ran while one was open for 10% -> 0% of each run, Pallas kernels for 39% -> 0%
where the time goes in v2:
time: 324 us; the launch traced here: 318 us
  Pallas kernels  267 us (82%)
  matrix products  25.7 us (8%)
  local copies, waits for them, and re-layouts  14 us (4%)
  other arithmetic  10.4 us (3%)
    pallas_call x1, Pallas kernels, attn_bwd(): pl.pallas_call(functools.partial(bwd_kernel, rows, merge), grid=(pairs,),...  119 us
    pallas_call x1, Pallas kernels, expert_pass(): pl.pallas_call(functools.partial(expert_kernel, groups, tile, n // 2), in...  98.2 us
    pallas_call x1, Pallas kernels, attn_fwd(): pl.pallas_call(functools.partial(fwd_kernel, rows), grid=(pairs,), in_spe...  45.7 us
    dot_general x9, matrix products, mm(): return lax.dot_general(a, b, dims, preferred_element_type=jnp.float32)  24.5 us

profile of v2, /device:TPU:0, one launch (start us, length us, event | category | flops | bytes accessed | tf_op | source)
XLA Modules:
  0.0 318.4 jit_solution(7352864790447931417)
XLA Ops:
  0.7 1.7 fusion.14
  2.5 4.2 %fusion.5 = bf16[1280,768]{1,0:T(8,128)(2,1)} fusion(bf16[1024,768]{1,0:T(8,128)(2,1)S(1)} %copy-done.14, s32[1024]{0:T(1024)S(1)} %bitcast.53), kind=kOutput, calls=%fused_computation.11 | convolution fusion | flops 2015559680 | bytes 3543040 | tf_op jit(solution)/shard_map/dot_general | solution.py:17
  7.2 2.6 convolution_convert_fusion.v_ref
  9.8 1.5 convolution_convert_fusion.1.k_ref
  11.3 2.6 convolution_convert_fusion.2.q_ref
  14.2 1.4 copy-done.3
  15.6 45.7 %attn_fwd.1 = (bf16[1024,768]{1,0:T(8,128)(2,1)S(1)}, bf16[12,1024,1024]{2,1,0:T(8,128)(2,1)}, bf16[16,80,768]{2,1,0:T(8,128)(2,1)}, bf16[8,80,768]{2,1,0:T(8,128)(2,1)S(1)}) custom-call(f32[6,2,512]{2,1,0:T(2,128)S(1)} %reshape.132.g_ref, bf16[1024,768]{1,0:T(8,128)(2,1)S(1)} %copy-done.3, bf16[1024,768]{1,0:T(8,128)(2,1)S(1)} %convolution_convert_fusion.1.k_ref, ...), custom_call_target="tpu_custom_call" | custom-call | tf_op jit(solution)/shard_map/attn_fwd/pallas_call | solution.py:341
  61.4 1.5 multiply_reduce_fusion.1
  63.0 0.6 fusion.29
  63.6 1.2 copy.62
  64.8 1.4 fusion.19
  66.2 2.3 fusion.16
  68.5 0.8 multiply_reduce_fusion
  69.4 0.6 broadcast_in_dim.73.gs_ref
  70.0 4.4 %fusion.6 = bf16[1280,768]{1,0:T(8,128)(2,1)} fusion(s32[1024]{0:T(1024)S(1)} %bitcast.55, f32[1024,768]{1,0:T(8,128)S(1)} %get-tuple-element.56.after_ref, f32[768]{0:T(1024)S(1)} %convert_element_type.97, f32[1024]{0:T(1024)S(1)} %add_rsqrt_fusion), kind=kOutput, calls=%fused_computation.12 | convolution fusion | flops 2017918976 | bytes 5123072 | tf_op jit(solution)/shard_map/dot_general | solution.py:17
  74.4 98.2 %experts.1 = (bf16[16,80,768]{2,1,0:T(8,128)(2,1)}, f32[16,8,128]{2,1,0:T(8,128)}, bf16[16,80,768]{2,1,0:T(8,128)(2,1)}, bf16[768,1536]{1,0:T(8,128)(2,1)}, bf16[1536,768]{1,0:T(8,128)(2,1)}) custom-call(bf16[16,80,768]{2,1,0:T(8,128)(2,1)} %bitcast.38, f32[16,8,128]{2,1,0:T(8,128)} %broadcast_in_dim.73.gs_ref, ...), custom_call_target="tpu_custom_call" | custom-call | tf_op jit(solution)/shard_map/experts/pallas_call | solution.py:235
  172.6 1.0 copy.63.stat_ref
  173.6 0.8 copy.64.wr_ref
  174.4 0.6 broadcast_in_dim.70.g1_ref
  175.0 0.6 broadcast_in_dim.71.g2_ref
  175.6 118.9 %attn_bwd.1 = (f32[1024,768]{1,0:T(8,128)}, f32[32,8,128]{2,1,0:T(8,128)}, bf16[6,32,96,128]{3,2,1,0:T(8,128)(2,1)}, bf16[16,80,768]{2,1,0:T(8,128)(2,1)}) custom-call(bf16[1024,768]{1,0:T(8,128)(2,1)} %convolution_convert_fusion.2.q_ref, bf16[1024,768]{1,0:T(8,128)(2,1)} %copy-done.2, bf16[1024,768]{1,0:T(8,128)(2,1)} %convolution_convert_fusion.v_ref, ...), custom_call_target="tpu_custom_call" | custom-call | tf_op jit(solution)/shard_map/attn_bwd/pallas_call | solution.py:693
  294.5 0.8 slice.46
  295.4 0.9 fusion.15
  296.3 2.3 copy-done.4
  298.6 4.3 %finish_sums.1 = (f32[768,768]{1,0:T(8,128)}, f32[768,768]{1,0:T(8,128)}, f32[768,768]{1,0:T(8,128)}, f32[768,768]{1,0:T(8,128)}) custom-call(bf16[6,4,768,128]{3,2,1,0:T(8,128)(2,1)S(1)} %bitcast.35), custom_call_target="tpu_custom_call" | custom-call | tf_op jit(solution)/shard_map/finish_sums/pallas_call | solution.py:730
  302.9 5.4 %add_convert_fusion = bf16[1024,768]{1,0:T(8,128)(2,1)} fusion(f32[1024,768]{1,0:T(8,128)S(1)} %copy-done.8, f32[1024]{0:T(1024)S(1)} %get-tuple-element.50, bf16[1280,768]{1,0:T(8,128)(2,1)} %bitcast.57, s32[1024]{0:T(1024)S(1)} %bitcast.56), kind=kOutput, calls=%fused_computation.16 | convolution fusion | flops 2016935936 | bytes 6692864 | tf_op jit(solution)/shard_map/dot_general | solution.py:17
  308.4 0.8 slice.51
  309.2 0.6 slice.44
  309.8 1.3 fusion.28
  311.1 2.5 bitcast_convert_fusion
  313.7 2.8 bitcast_convert_fusion.1
  316.5 1.7 copy.68
  (63 shorter events, 1.1 us)
Async XLA Ops:
  0.6 13.3 %copy-start = (bf16[32,12]{0,1:T(8,128)(2,1)S(1)}, bf16[32,12]{0,1:T(8,128)(2,1)}, u32[]{:S(2)}) copy-start(bf16[32,12]{0,1:T(8,128)(2,1)} %param.23) | copy-start | bytes 2308
  0.7 1.8 copy-start.22
  0.7 1.8 copy-start.14
  2.5 4.3 %copy-start.9 = (bf16[1024,768]{1,0:T(8,128)(2,1)S(1)}, bf16[1024,768]{1,0:T(8,128)(2,1)}, u32[]{:S(2)}) copy-start(bf16[1024,768]{1,0:T(8,128)(2,1)} %tok_ref.1) | copy-start | bytes 4718596
  2.5 4.6 %copy-start.23 = (bf16[768]{0:T(1024)(128)(2,1)S(1)}, bf16[768]{0:T(1024)(128)(2,1)}, u32[]{:S(2)}) copy-start(bf16[768]{0:T(1024)(128)(2,1)} %param.18) | copy-start | bytes 4612
  2.5 4.6 %copy-start.17 = (bf16[768,768]{1,0:T(8,128)(2,1)S(1)}, bf16[768,768]{1,0:T(8,128)(2,1)}, u32[]{:S(2)}) copy-start(bf16[768,768]{1,0:T(8,128)(2,1)} %wv_ref.1) | copy-start | bytes 3538948
  7.1 2.6 copy-start.16
  9.8 1.5 copy-start.15
  11.2 2.9 copy-start.2
  11.3 2.6 copy-start.20
  14.2 1.4 copy-start.3
  15.6 45.7 %copy-start.10 = (bf16[1024,768]{1,0:T(8,128)(2,1)S(1)}, bf16[1024,768]{1,0:T(8,128)(2,1)}, u32[]{:S(2)}) copy-start(bf16[1024,768]{1,0:T(8,128)(2,1)} %tok_ref.1) | copy-start | bytes 4718596
  15.6 45.8 %copy-start.18 = (bf16[768,768]{1,0:T(8,128)(2,1)S(1)}, bf16[768,768]{1,0:T(8,128)(2,1)}, u32[]{:S(2)}) copy-start(bf16[768,768]{1,0:T(8,128)(2,1)} %wo_ref.1) | copy-start | bytes 3538948
  61.3 1.6 copy-start.5
  61.3 1.6 copy-start.6
  61.4 1.6 copy-start.24
  61.4 1.6 copy-start.21
  62.9 7.1 %copy-start.7 = (f32[1024,768]{1,0:T(8,128)}, f32[1024,768]{1,0:T(8,128)S(1)}, u32[]{:S(2)}) copy-start(f32[1024,768]{1,0:T(8,128)S(1)} %get-tuple-element.56.after_ref) | copy-start | bytes 9437188
  175.6 119.8 %copy-start.19 = (f32[512,32]{1,0:T(8,128)S(1)}, f32[512,32]{1,0:T(8,128)}, u32[]{:S(2)}) copy-start(f32[512,32]{1,0:T(8,128)} %constant.26.clone) | copy-start | bytes 196612
  296.3 2.3 copy-start.4
  298.6 4.3 %copy-start.8 = (f32[1024,768]{1,0:T(8,128)S(1)}, f32[1024,768]{1,0:T(8,128)}, u32[]{:S(2)}) copy-start(f32[1024,768]{1,0:T(8,128)} %copy-done.7) | copy-start | bytes 9437188
  302.9 8.2 %copy-start.13 = (bf16[1536,768]{1,0:T(8,128)(2,1)S(1)}, bf16[1536,768]{1,0:T(8,128)(2,1)}, u32[]{:S(2)}) copy-start(bf16[1536,768]{1,0:T(8,128)(2,1)} %get-tuple-element.45) | copy-start | bytes 7077892
  311.1 2.6 copy-start.12
  313.7 2.8 copy-start.11
  313.7 4.5 %copy-start.1 = (bf16[32,12]{0,1:T(8,128)(2,1)S(1)}, bf16[32,12]{0,1:T(8,128)(2,1)}, u32[]{:S(2)}) copy-start(bf16[32,12]{0,1:T(8,128)(2,1)} %param.23) | copy-start | bytes 2308
